TPU v7x, 32 devices: a whole 2x2x4 slice. The times are simulated.
32 devices in a mesh: space: 8 (over y, x, core), level: 4 (over z).
Axes of the slice: x: 2, y: 2, z: 4, core: 2. Of those that a mesh axis runs over, the one named last changes fastest.
Arguments:
- fields: bfloat16 [4, 4096, 768], P('level', 'space'), may hold values from -16 to 16
- norm_vert: float32 [768], replicated, may hold values from 0.1 to 1.9
- query_vert: bfloat16 [768, 768], replicated, may hold values from -0.21875 to 0.21875
- keys_vert: bfloat16 [768, 768], replicated, may hold values from -0.21875 to 0.21875
- values_vert: bfloat16 [768, 768], replicated, may hold values from -0.21875 to 0.21875
- out_vert: bfloat16 [768, 768], replicated, may hold values from -0.21875 to 0.21875
- level_bias: float32 [12, 4, 4], replicated, may hold values from -3 to 250
- norm_patch: float32 [768], replicated, may hold values from 0.1 to 1.9
- query_patch: bfloat16 [768, 768], replicated, may hold values from -0.21875 to 0.21875
- keys_patch: bfloat16 [768, 768], replicated, may hold values from -0.21875 to 0.21875
- values_patch: bfloat16 [768, 768], replicated, may hold values from -0.21875 to 0.21875
- out_patch: bfloat16 [768, 768], replicated, may hold values from -0.21875 to 0.21875
- patch_bias: float32 [12, 2], replicated, may hold values from -3 to 250
- neighbours: int32 [16, 4], P('space'), may hold values from -1 to 15, as said below
- counts: int32 [16], P('space'), may hold values from 2 to 4, as said below
- cotangent: bfloat16 [4, 4096, 768], P('level', 'space'), may hold values from -0.046875 to 0.046875
Outputs:
- out_fields: bfloat16 [4, 4096, 768], P('level', 'space')
- grad_wo: float32 [768, 768], P('space')
Inputs may be any that keep to these rules, and one draw needn't show every extreme that they name: `neighbours`: row p lists distinct patches, at most one from each device of space, held on devices at cycle distance 1 to 2 from the device of patch p (device s of space holds patches s * 2 to (s + 1) * 2 - 1); entries from counts[p] on are -1. `counts`: some patch has 4 neighbours in every draw.
All inputs are finite; a program needn't handle non-finite values.
Results may differ from a plain program's by a relative error of at most 0.025.
Values may be sent and summed in bfloat16 or wider, within the bound.
A program may use at most 128 MiB of HBM per device.

v0:
```python
import jax
import jax.numpy as jnp
from jax import lax
from jax.sharding import PartitionSpec as P

H = 12
HD = 64
PATCH = 256
REACH = 2


epsilon = 1e-06


def passed_along(value, axis, steps):
    count = lax.axis_size(axis)
    pairs = [(source, (source + steps) % count) for source in range(count)]
    return lax.ppermute(value, axis, pairs)


def normalize(values, scaling):
    widened = values.astype(jnp.float32)
    mean_square = jnp.mean(widened * widened, axis=-1, keepdims=True)
    return (widened * lax.rsqrt(mean_square + epsilon) * scaling).astype(jnp.bfloat16)


def project(inputs, weight):
    return jnp.dot(inputs, weight, preferred_element_type=jnp.float32).astype(jnp.bfloat16)


def vertical_heads(queries, keys_in, values_in, bias_table):
    level_count, columns, features = queries.shape
    query_heads = queries.reshape(level_count, columns, H, HD)
    key_heads = keys_in.reshape(keys_in.shape[0], columns, H, HD)
    value_heads = values_in.reshape(values_in.shape[0], columns, H, HD)
    scores = (
        jnp.einsum("ichd,jchd->hijc", query_heads, key_heads, preferred_element_type=jnp.float32)
        * HD ** (-0.5)
        + bias_table[:, :, :, None]
    )
    weights = jax.nn.softmax(scores, axis=2).astype(jnp.bfloat16)
    mixture = jnp.einsum(
        "hijc,jchd->ichd", weights, value_heads, preferred_element_type=jnp.float32
    )
    return mixture.astype(jnp.bfloat16).reshape(level_count, columns, features)


def patch_heads(queries, own_keys, nearby, live_count, bias_table):
    features = queries.shape[-1]
    patch_len = own_keys.shape[0]
    keys_all = jnp.concatenate((own_keys[None], nearby), axis=0).reshape(-1, 2 * features)
    query_heads = queries.reshape(-1, H, HD)
    key_heads = keys_all[:, :features].reshape(-1, H, HD)
    value_heads = keys_all[:, features:].reshape(-1, H, HD)
    scores = jnp.einsum(
        "qhd,khd->hqk", query_heads, key_heads, preferred_element_type=jnp.float32
    ) * HD ** (-0.5)
    block_bias = jnp.concatenate(
        (bias_table[:, :1], jnp.broadcast_to(bias_table[:, 1:], (H, nearby.shape[0]))), axis=1
    )
    scores = scores + jnp.repeat(block_bias, patch_len, axis=1)[:, None, :]
    opened = jnp.repeat(jnp.arange(nearby.shape[0] + 1, dtype=jnp.int32) <= live_count, patch_len)
    scores = jnp.where(opened[None, None, :], scores, -jnp.inf)
    weights = jax.nn.softmax(scores, axis=-1).astype(jnp.bfloat16)
    mixture = jnp.einsum("hqk,khd->qhd", weights, value_heads, preferred_element_type=jnp.float32)
    return mixture.astype(jnp.bfloat16).reshape(-1, features)


def body(
    fields,
    norm_vert,
    query_vert,
    keys_vert,
    values_vert,
    out_vert,
    level_bias,
    norm_patch,
    query_patch,
    keys_patch,
    values_patch,
    out_patch,
    patch_bias,
    neighbours,
    counts,
    cotangent,
):
    level_count, columns, features = fields.shape
    groups = lax.axis_size("level")
    normed = normalize(fields, norm_vert)
    vertical_in = jnp.concatenate((query_vert, keys_vert, values_vert), axis=1)
    projected = project(normed, vertical_in)
    split_in = projected.reshape(level_count, groups, columns // groups, 3 * features)
    merged = lax.all_to_all(split_in, "level", split_axis=1, concat_axis=0, tiled=True)[:, 0]
    result = vertical_heads(
        merged[..., :features],
        merged[..., features : 2 * features],
        merged[..., 2 * features :],
        level_bias,
    )
    mixture = result[:, None]
    attn_vert = lax.all_to_all(mixture, "level", split_axis=0, concat_axis=1, tiled=True).reshape(
        level_count, columns, features
    )
    hidden = (
        fields.astype(jnp.float32)
        + jnp.dot(attn_vert, out_vert, preferred_element_type=jnp.float32)
    ).astype(jnp.bfloat16)
    pair_in = jnp.concatenate((keys_patch, values_patch), axis=1)
    normed_patch = normalize(hidden, norm_patch)
    queries_patch = project(normed_patch, query_patch)
    key_values = project(normed_patch, pair_in)
    offsets = [stride for stride in range(1, REACH + 1)] + [
        -stride for stride in range(1, REACH + 1)
    ]
    arrived = [passed_along(normed_patch, "space", offset) for offset in offsets]
    distant = project(jnp.stack(arrived), pair_in)
    per_device = columns // PATCH
    distant = distant.reshape(2 * REACH, level_count, per_device, PATCH, 2 * features)
    position = lax.axis_index("space")
    cycle_size = lax.axis_size("space")
    clipped = jnp.maximum(neighbours, 0)
    owner = clipped // per_device
    distance = (position - owner) % cycle_size
    source = jnp.where(distance <= REACH, distance - 1, REACH + cycle_size - distance - 1)
    source = jnp.clip(source, 0, 2 * REACH - 1)
    within = clipped % per_device

    def level_mix(query_level, own_level, distant_level):
        nearby = distant_level[source, within]
        return jax.vmap(patch_heads, in_axes=(0, 0, 0, 0, None))(
            query_level, own_level, nearby, counts, patch_bias
        )

    mixture_patch = jax.vmap(level_mix, in_axes=(0, 0, 1))(
        queries_patch.reshape(level_count, per_device, PATCH, features),
        key_values.reshape(level_count, per_device, PATCH, 2 * features),
        distant,
    )
    attn_patch = mixture_patch.reshape(level_count, columns, features)
    out_fields = (
        hidden.astype(jnp.float32)
        + jnp.dot(attn_patch, out_patch, preferred_element_type=jnp.float32)
    ).astype(jnp.bfloat16)
    flat_attn = attn_patch.reshape(-1, features)
    flat_cotangent = cotangent.reshape(-1, features)
    shares = lax.psum_scatter(
        lax.dot_general(
            flat_attn, flat_cotangent, (((0,), (0,)), ((), ())), preferred_element_type=jnp.float32
        ).astype(jnp.bfloat16),
        "space",
        scatter_dimension=0,
        tiled=True,
    )
    grad_wo = lax.psum(shares, "level").astype(jnp.float32)
    return (out_fields, grad_wo)


def solution(mesh):
    return jax.shard_map(
        body,
        mesh=mesh,
        in_specs=(
            P("level", "space", None),
            P(),
            P(),
            P(),
            P(),
            P(),
            P(),
            P(),
            P(),
            P(),
            P(),
            P(),
            P(),
            P("space", None),
            P("space"),
            P("level", "space", None),
        ),
        out_specs=(P("level", "space", None), P("space", None)),
        check_vma=False,
    )
```

profile of v0, /device:TPU:0, one launch (start us, length us, event | category | flops | bytes accessed | tf_op | source)
XLA Modules:
  0.0 335.4 jit_solution(17246680369269153822)
XLA Ops:
  7.2 0.0 copy-start
  7.2 1.5 fusion.23
  8.6 4.3 %convolution_convert_fusion.1 = bf16[512,2304]{1,0:T(8,128)(2,1)S(1)} fusion(bf16[768,768]{1,0:T(8,128)(2,1)} %param.20, bf16[768,768]{1,0:T(8,128)(2,1)} %param.19, bf16[768,768]{1,0:T(8,128)(2,1)} %param.18, bf16[1,512,768]{2,1,0:T(8,128)(2,1)} %param.16, f32[768]{0:T(1024)} %param.17, f32[512]{0:T(512)S(1)} %add_rsqrt_fusion.1), kind=kOutput, calls=%fused_computation.15 | convolution fusion | flops 1825308672 | bytes 6689792 | tf_op jit(solution)/shard_map/dot_general | solution.py:28
  13.0 2.5 copy.53
  15.5 6.5 %all-to-all-start = ((bf16[1,4,128,2304]{2,3,0,1:T(8,128)(2,1)}), bf16[1,4,128,2304]{2,3,0,1:T(8,128)(2,1)S(1)}, u32[]{:S(2)}, u32[]{:S(2)}) async-start(bf16[1,4,128,2304]{2,3,0,1:T(8,128)(2,1)} %copy.53), calls=%async_computation | async-start | bytes 4718592 | tf_op jit(solution)/shard_map/all_to_all | solution.py:93
  21.9 0.7 copy.56
  22.6 53.1 %all-to-all-done = bf16[1,4,128,2304]{2,3,0,1:T(8,128)(2,1)S(1)} async-done(((bf16[1,4,128,2304]{2,3,0,1:T(8,128)(2,1)}), bf16[1,4,128,2304]{2,3,0,1:T(8,128)(2,1)S(1)}, u32[]{:S(2)}, u32[]{:S(2)}) %all-to-all-start) | async-done | bytes 2359328 | tf_op jit(solution)/shard_map/all_to_all | solution.py:93
  75.7 1.5 fusion.61
  77.2 3.6 %copy.54 = bf16[4,128,12,64]{3,0,1,2:T(4,128)(2,1)} copy(bf16[4,128,12,64]{1,3,2,0:T(8,128)(2,1)} %bitcast.90) | data formatting | bytes 1572864 | tf_op jit(solution)/shard_map/reshape | solution.py:34
  80.8 2.2 copy.55
  83.0 2.5 copy.57
  85.5 9.0 %fusion.63 = (f32[12,4,128]{1,2,0:T(8,128)}, f32[12,4,4,128]{1,2,3,0:T(4,128)}) fusion(f32[12,4,4]{1,2,0:T(4,128)} %copy.56, bf16[4,128,12,64]{3,0,1,2:T(4,128)(2,1)S(1)} %copy-done.4, bf16[4,128,12,64]{3,0,1,2:T(4,128)(2,1)} %copy.55), kind=kOutput, calls=%fused_computation.94 | convolution fusion | flops 3244035 | bytes 1696512 | tf_op jit(solution)/shard_map/sub | solution.py:41
  94.5 4.0 %fusion.34 = bf16[4,128,12,64]{3,0,2,1:T(4,128)(2,1)S(1)} fusion(bf16[4,128,12,64]{3,0,2,1:T(4,128)(2,1)} %copy.57, f32[12,4,4,128]{1,2,3,0:T(4,128)} %get-tuple-element.10, f32[12,4,128]{1,2,0:T(8,128)} %get-tuple-element.9), kind=kOutput, calls=%fused_computation.53 | convolution fusion | flops 3588096 | bytes 1695744 | tf_op jit(solution)/shard_map/hijc,jchd->ichd/dot_general | solution.py:42
  98.4 0.0 copy-start.14
  98.5 0.0 copy-start.18
  98.5 2.3 copy.59
  100.8 3.6 %all-to-all-start.1 = ((bf16[4,1,128,768]{2,3,1,0:T(8,128)(2,1)}), bf16[4,1,128,768]{2,3,1,0:T(8,128)(2,1)S(1)}, u32[]{:S(2)}, u32[]{:S(2)}) async-start(bf16[4,1,128,768]{2,3,1,0:T(8,128)(2,1)} %bitcast.9), calls=%async_computation.1 | async-start | bytes 1572864 | tf_op jit(solution)/shard_map/all_to_all | solution.py:101
  104.4 0.2 reduce-scatter.2.cloned.1.call-start
  104.7 0.1 reshape.163
  104.8 0.1 iota_compare_fusion
  104.9 0.1 broadcast_bitcast_fusion
  105.0 0.1 copy.67
  105.1 0.1 broadcast_in_dim.50
  105.2 0.1 pad_maximum_fusion.1
  105.2 0.1 broadcast_in_dim.51
  105.3 0.7 copy.72
  106.0 1.2 constant_dynamic-update-slice_fusion.1
  107.2 16.9 %all-to-all-done.1 = bf16[4,1,128,768]{2,3,1,0:T(8,128)(2,1)S(1)} async-done(((bf16[4,1,128,768]{2,3,1,0:T(8,128)(2,1)}), bf16[4,1,128,768]{2,3,1,0:T(8,128)(2,1)S(1)}, u32[]{:S(2)}, u32[]{:S(2)}) %all-to-all-start.1) | async-done | bytes 786464 | tf_op jit(solution)/shard_map/all_to_all | solution.py:101
  124.1 0.3 copy.61
  124.4 0.0 copy-start.13
  124.4 0.0 copy-start.6
  124.4 2.2 fusion.27
  126.6 1.1 fusion.29
  127.7 2.4 collective-permute-start.3
  130.2 0.5 collective-permute-start.1
  130.7 0.1 collective-permute-start
  130.7 0.1 constant_dynamic-update-slice_fusion
  130.8 1.4 copy-done.9
  132.2 1.9 convolution_convert_fusion.5
  134.2 0.3 copy.64
  134.4 1.1 reshape.157
  135.5 3.4 %convolution_convert_fusion.2 = bf16[512,1536]{1,0:T(8,128)(2,1)S(1)} fusion(bf16[768,1536]{1,0:T(8,128)(2,1)} %copy-done.9, bf16[1,512,768]{2,1,0:T(8,128)(2,1)} %fusion.29), kind=kOutput, calls=%fused_computation.31 | convolution fusion | flops 1208745984 | bytes 4718592 | tf_op jit(solution)/shard_map/dot_general | solution.py:28
  139.0 9.5 %collective-permute-done.3 = bf16[1,512,768]{2,1,0:T(8,128)(2,1)} collective-permute-done((bf16[1,512,768]{2,1,0:T(8,128)(2,1)}, bf16[1,512,768]{2,1,0:T(8,128)(2,1)}, u32[]{:S(2)}, u32[]{:S(2)}) %collective-permute-start.3) | collective-permute-done | bytes 786464 | tf_op jit(solution)/shard_map/ppermute | solution.py:18
  148.5 16.8 %collective-permute-done.2 = bf16[1,512,768]{2,1,0:T(8,128)(2,1)} collective-permute-done((bf16[1,512,768]{2,1,0:T(8,128)(2,1)}, bf16[1,512,768]{2,1,0:T(8,128)(2,1)}, u32[]{:S(2)}, u32[]{:S(2)}) %collective-permute-start.2) | collective-permute-done | bytes 786464 | tf_op jit(solution)/shard_map/ppermute | solution.py:18
  165.3 16.0 %collective-permute-done.1 = bf16[1,512,768]{2,1,0:T(8,128)(2,1)} collective-permute-done((bf16[1,512,768]{2,1,0:T(8,128)(2,1)}, bf16[1,512,768]{2,1,0:T(8,128)(2,1)}, u32[]{:S(2)}, u32[]{:S(2)}) %collective-permute-start.1) | collective-permute-done | bytes 786464 | tf_op jit(solution)/shard_map/ppermute | solution.py:18
  181.3 8.9 %convolution_convert_fusion = bf16[4,512,1536]{2,1,0:T(8,128)(2,1)} fusion(bf16[1,1,512,768]{3,2,1,0:T(8,128)(2,1)} %bitcast.18, bf16[1,1,512,768]{3,2,1,0:T(8,128)(2,1)} %bitcast.17, bf16[1,1,512,768]{3,2,1,0:T(8,128)(2,1)} %bitcast.16, bf16[1,1,512,768]{3,2,1,0:T(8,128)(2,1)} %bitcast.15, bf16[768,1536]{1,0:T(8,128)(2,1)S(1)} %copy-done.10), kind=kOutput, calls=%fused_computation.13 | convolution fusion | flops 4839702528 | bytes 11796480 | tf_op jit(solution)/shard_map/dot_general | solution.py:28
  190.2 6.4 %gather_fusion = bf16[8,256,1536]{2,1,0:T(8,128)(2,1)} fusion(bf16[4,2,256,1536]{3,2,1,0:T(8,128)(2,1)} %bitcast.85, s32[8]{0:T(128)S(1)} %reshape.163), kind=kCustom, calls=%fused_computation | custom fusion | bytes 12582976 | tf_op jit(solution)/shard_map/vmap()/gather | solution.py:129
  196.7 6.5 %pad_maximum_fusion = bf16[1,2,5,256,1536]{4,3,2,1,0:T(8,128)(2,1)} fusion(bf16[1,2,4,256,1536]{4,3,2,1,0:T(8,128)(2,1)} %bitcast.83, bf16[1,2,1,256,1536]{4,3,2,1,0:T(8,128)(2,1)S(1)} %bitcast.93), kind=kLoop, calls=%fused_computation.12 | loop fusion | flops 3932160 | bytes 15728640 | tf_op jit(solution)/shard_map/vmap(vmap())/concatenate | solution.py:51
  203.2 5.4 %fusion.60 = (bf16[1,2,1280,768]{3,2,1,0:T(8,128)(2,1)}, bf16[1,2,1280,768]{3,2,1,0:T(8,128)(2,1)}) fusion(bf16[1,2,1280,1536]{3,2,1,0:T(8,128)(2,1)} %bitcast.82), kind=kLoop, calls=%fused_computation.91 | loop fusion | bytes 15728640 | tf_op jit(solution)/shard_map/vmap(vmap())/slice | solution.py:53
  208.6 6.3 %copy.65 = bf16[1,2,1280,768]{2,3,1,0:T(8,128)(2,1)} copy(bf16[1,2,1280,768]{3,2,1,0:T(8,128)(2,1)} %get-tuple-element.2) | data formatting | bytes 7864320 | tf_op jit(solution)/shard_map/vmap(vmap())/slice | solution.py:53
  214.9 6.4 %copy.63 = bf16[1,2,1280,768]{2,3,1,0:T(8,128)(2,1)} copy(bf16[1,2,1280,768]{3,2,1,0:T(8,128)(2,1)} %get-tuple-element.3) | data formatting | bytes 7864320 | tf_op jit(solution)/shard_map/vmap(vmap())/slice | solution.py:54
  221.3 17.4 %fusion.64 = (f32[2,12,256]{2,1,0:T(8,128)S(1)}, f32[2,12,256,1280]{3,2,1,0:T(8,128)}) fusion(f32[12,1280]{1,0:T(8,128)S(1)} %bitcast.98, pred[2,1280]{1,0:T(4,128)(4,1)S(1)} %bitcast.99, bf16[2,1280,12,64]{1,3,2,0:T(8,128)(2,1)} %bitcast.86, bf16[2,256,12,64]{1,0,3,2:T(2,128)(2,1)S(1)} %copy-done.7), kind=kOutput, calls=%fused_computation.95 | convolution fusion | flops 1045955840 | bytes 36264448 | tf_op jit(solution)/shard_map/vmap(vmap())/sub | solution.py:64
  238.7 14.3 %fusion.38 = bf16[1,2,256,12,64]{2,4,3,1,0:T(8,128)(2,1)S(1)} fusion(bf16[2,1280,12,64]{1,3,2,0:T(8,128)(2,1)} %bitcast.87, f32[2,12,256,1280]{3,2,1,0:T(8,128)} %get-tuple-element.14, f32[2,12,256]{2,1,0:T(8,128)S(1)} %get-tuple-element.13), kind=kOutput, calls=%fused_computation.56 | convolution fusion | flops 1022754816 | bytes 36200448 | tf_op jit(solution)/shard_map/vmap(vmap(hqk,khd->qhd))/dot_general | solution.py:65
  253.0 0.8 copy.68
  253.8 0.2 copy.73
  254.0 0.1 copy-done.17
  254.1 1.8 convolution_convert_fusion.4
  256.0 0.0 reduce-scatter.2.cloned.1.call-update
  256.0 0.0 all-reduce.2.cloned.1.call-start
  256.0 34.1 %reduce-scatter.2.cloned.1.call-done = bf16[96,768]{1,0:T(8,128)(2,1)} async-done(((bf16[768,768]{1,0:T(8,128)(2,1)}), bf16[96,768]{1,0:T(8,128)(2,1)}) %reduce-scatter.2.cloned.1.call-update) | async-done | bytes 147472 | tf_op jit(solution)/shard_map/reduce_scatter | solution.py:146
  290.1 0.0 all-reduce.2.cloned.1.call-update
  290.2 3.1 fusion.30
  293.2 33.7 %all-reduce.2.cloned.1.call-done = bf16[96,768]{1,0:T(8,128)(2,1)} async-done(((bf16[96,768]{1,0:T(8,128)(2,1)}), bf16[96,768]{1,0:T(8,128)(2,1)}) %all-reduce.2.cloned.1.call-update) | async-done | bytes 147472 | tf_op jit(solution)/shard_map/psum | solution.py:154
  327.0 1.6 convert_element_type.82
  (39 shorter events, 0.1 us)
Async XLA Ops:
  7.2 117.2 %copy-start = (bf16[768,768]{1,0:T(8,128)(2,1)S(1)}, bf16[768,768]{1,0:T(8,128)(2,1)}, u32[]{:S(2)}) copy-start(bf16[768,768]{1,0:T(8,128)(2,1)} %param.21) | copy-start | bytes 3538948
  15.5 6.5 %copy-start.12 = (f32[12,4,4]{0,2,1:T(4,128)S(1)}, f32[12,4,4]{0,2,1:T(4,128)}, u32[]{:S(2)}) copy-start(f32[12,4,4]{0,2,1:T(4,128)} %param.22) | copy-start | bytes 2308
  15.5 60.3 %all-to-all-start = ((bf16[1,4,128,2304]{2,3,0,1:T(8,128)(2,1)}), bf16[1,4,128,2304]{2,3,0,1:T(8,128)(2,1)S(1)}, u32[]{:S(2)}, u32[]{:S(2)}) async-start(bf16[1,4,128,2304]{2,3,0,1:T(8,128)(2,1)} %copy.53), calls=%async_computation | async-start | bytes 4718592 | tf_op jit(solution)/shard_map/all_to_all | solution.py:93
  77.2 3.6 %copy-start.3 = (bf16[4,128,768]{1,2,0:T(8,128)(2,1)S(1)}, bf16[4,128,768]{1,2,0:T(8,128)(2,1)}, u32[]{:S(2)}) copy-start(bf16[4,128,768]{1,2,0:T(8,128)(2,1)} %get-tuple-element.4) | copy-start | bytes 2359300
  77.2 5.7 %copy-start.2 = (bf16[4,128,768]{1,2,0:T(8,128)(2,1)S(1)}, bf16[4,128,768]{1,2,0:T(8,128)(2,1)}, u32[]{:S(2)}) copy-start(bf16[4,128,768]{1,2,0:T(8,128)(2,1)} %get-tuple-element.6) | copy-start | bytes 2359300
  83.0 2.5 copy-start.4
  98.4 6.2 %copy-start.14 = (s32[2,4]{1,0:T(2,128)S(1)}, s32[2,4]{1,0:T(2,128)}, u32[]{:S(2)}) copy-start(s32[2,4]{1,0:T(2,128)} %param.29) | copy-start | bytes 100
  98.5 6.3 %copy-start.18 = (s32[2]{0:T(128)S(1)}, s32[2]{0:T(128)}, u32[]{:S(2)}) copy-start(s32[2]{0:T(128)} %param.30) | copy-start | bytes 28
  98.5 6.5 %copy-start.15 = (f32[12,2]{0,1:T(2,128)S(1)}, f32[12,2]{0,1:T(2,128)}, u32[]{:S(2)}) copy-start(f32[12,2]{0,1:T(2,128)} %param.28) | copy-start | bytes 292
  100.8 5.2 %copy-start.5 = (bf16[768,768]{1,0:T(8,128)(2,1)S(1)}, bf16[768,768]{1,0:T(8,128)(2,1)}, u32[]{:S(2)}) copy-start(bf16[768,768]{1,0:T(8,128)(2,1)} %param.25) | copy-start | bytes 3538948
  100.8 23.3 %all-to-all-start.1 = ((bf16[4,1,128,768]{2,3,1,0:T(8,128)(2,1)}), bf16[4,1,128,768]{2,3,1,0:T(8,128)(2,1)S(1)}, u32[]{:S(2)}, u32[]{:S(2)}) async-start(bf16[4,1,128,768]{2,3,1,0:T(8,128)(2,1)} %bitcast.9), calls=%async_computation.1 | async-start | bytes 1572864 | tf_op jit(solution)/shard_map/all_to_all | solution.py:101
  104.4 185.7 %reduce-scatter.2.cloned.1.call-start = ((), (), s32[]{:S(2)}) async-start(), calls=%async_computation.3 | async-start | bytes 1327104 | tf_op jit(solution)/shard_map/reduce_scatter | solution.py:146
  124.4 2.2 copy-start.13
  124.4 6.3 %copy-start.6 = (bf16[768,768]{1,0:T(8,128)(2,1)S(1)}, bf16[768,768]{1,0:T(8,128)(2,1)}, u32[]{:S(2)}) copy-start(bf16[768,768]{1,0:T(8,128)(2,1)} %param.26) | copy-start | bytes 3538948
  124.4 6.3 %copy-start.8 = (bf16[768,1536]{1,0:T(8,128)(2,1)S(1)}, bf16[768,1536]{1,0:T(8,128)(2,1)}, u32[]{:S(2)}) copy-start(bf16[768,1536]{1,0:T(8,128)(2,1)} %constant_dynamic-update-slice_fusion.1) | copy-start | bytes 7077892
  126.6 5.6 %copy-start.16 = (bf16[768,768]{1,0:T(8,128)(2,1)S(1)}, bf16[768,768]{1,0:T(8,128)(2,1)}, u32[]{:S(2)}) copy-start(bf16[768,768]{1,0:T(8,128)(2,1)} %param.24) | copy-start | bytes 3538948
  127.7 20.7 %collective-permute-start.3 = (bf16[1,512,768]{2,1,0:T(8,128)(2,1)}, bf16[1,512,768]{2,1,0:T(8,128)(2,1)}, u32[]{:S(2)}, u32[]{:S(2)}) collective-permute-start(bf16[1,512,768]{2,1,0:T(8,128)(2,1)} %fusion.29), channel_id=1, source_target_pairs={{0,24},{4,28},{8,0},{12,4},{16,8},{20,12},{24,16},{28,20},{1,25},{... | collective-permute-start | bytes 2359304 | tf_op jit(solution)/shard_map/ppermute | solution.py:18
  130.2 35.1 %collective-permute-start.2 = (bf16[1,512,768]{2,1,0:T(8,128)(2,1)}, bf16[1,512,768]{2,1,0:T(8,128)(2,1)}, u32[]{:S(2)}, u32[]{:S(2)}) collective-permute-start(bf16[1,512,768]{2,1,0:T(8,128)(2,1)} %fusion.29), channel_id=1, source_target_pairs={{0,28},{4,0},{8,4},{12,8},{16,12},{20,16},{24,20},{28,24},{1,29},{... | collective-permute-start | bytes 2359304 | tf_op jit(solution)/shard_map/ppermute | solution.py:18
  130.2 51.1 %collective-permute-start.1 = (bf16[1,512,768]{2,1,0:T(8,128)(2,1)}, bf16[1,512,768]{2,1,0:T(8,128)(2,1)}, u32[]{:S(2)}, u32[]{:S(2)}) collective-permute-start(bf16[1,512,768]{2,1,0:T(8,128)(2,1)} %fusion.29), channel_id=1, source_target_pairs={{0,8},{4,12},{8,16},{12,20},{16,24},{20,28},{24,0},{28,4},{1,9},{5... | collective-permute-start | bytes 2359304 | tf_op jit(solution)/shard_map/ppermute | solution.py:18
  130.7 50.6 %collective-permute-start = (bf16[1,512,768]{2,1,0:T(8,128)(2,1)}, bf16[1,512,768]{2,1,0:T(8,128)(2,1)}, u32[]{:S(2)}, u32[]{:S(2)}) collective-permute-start(bf16[1,512,768]{2,1,0:T(8,128)(2,1)} %fusion.29), channel_id=1, source_target_pairs={{0,4},{4,8},{8,12},{12,16},{16,20},{20,24},{24,28},{28,0},{1,5},{5... | collective-permute-start | bytes 2359304 | tf_op jit(solution)/shard_map/ppermute | solution.py:18
  130.8 1.4 copy-start.9
  135.5 45.8 %copy-start.10 = (bf16[768,1536]{1,0:T(8,128)(2,1)S(1)}, bf16[768,1536]{1,0:T(8,128)(2,1)}, u32[]{:S(2)}) copy-start(bf16[768,1536]{1,0:T(8,128)(2,1)} %copy-done.9) | copy-start | bytes 7077892
  214.9 6.4 %copy-start.7 = (bf16[2,256,12,64]{1,0,3,2:T(2,128)(2,1)S(1)}, bf16[2,256,12,64]{1,0,3,2:T(2,128)(2,1)}, u32[]{:S(2)}) copy-start(bf16[2,256,12,64]{1,0,3,2:T(2,128)(2,1)} %reshape.157) | copy-start | bytes 2359300
  214.9 6.4 %copy-start.11 = (f32[2,8,5,256]{3,1,2,0:T(8,128)S(1)}, f32[2,8,5,256]{3,1,2,0:T(8,128)}, u32[]{:S(2)}) copy-start(f32[2,8,5,256]{3,1,2,0:T(8,128)} %copy.72) | copy-start | bytes 245764
  253.0 1.1 copy-start.17
  256.0 71.0 %all-reduce.2.cloned.1.call-start = ((), (), s32[]{:S(2)}) async-start(), calls=%async_computation.4 | async-start | bytes 294912 | tf_op jit(solution)/shard_map/psum | solution.py:154
  290.1 38.5 %copy-start.1 = (bf16[768,768]{1,0:T(8,128)(2,1)S(1)}, bf16[768,768]{1,0:T(8,128)(2,1)}, u32[]{:S(2)}) copy-start(bf16[768,768]{1,0:T(8,128)(2,1)} %param.21) | copy-start | bytes 3538948
Sparse Core Ops, SparseCore 0:
  256.1 33.9 reduce-scatter.1
  292.4 34.4 all-reduce.1
where the time goes:
time: 336 us; the launch traced here: 335 us
  waiting for transfers between devices  180 us (54%)
  matrix products  70.3 us (21%)
  local copies, waits for them, and re-layouts  46.4 us (14%)
  between operations  14.3 us (4%)
  starting transfers between devices  13.3 us (4%)
  other arithmetic  10.9 us (3%)
    all_to_all x1, waiting for transfers between devices, body(): lax.all_to_all(split_in, 'level', split_axis=1, concat_axis=0, tiled=True)  53.1 us
    ppermute x4, waiting for transfers between devices, passed_along(): return lax.ppermute(value, axis, pairs)  42.3 us
    reduce_scatter x1, waiting for transfers between devices, body(): lax.psum_scatter(lax.dot_general(flat_attn, flat_cotangent, (((0,), (0,))...  34.1 us
    psum x1, waiting for transfers between devices, body(): grad_wo = lax.psum(shares, 'level').astype(jnp.float32)  33.7 us
    dot_general x4, matrix products, project(): jnp.dot(inputs, weight, preferred_element_type=jnp.float32)  18.6 us
    sub x1, matrix products, patch_heads(): weights = jax.nn.softmax(scores, axis=-1).astype(jnp.bfloat16)  17.4 us
    all_to_all x1, waiting for transfers between devices, body(): lax.all_to_all(mixture, 'level', split_axis=0, concat_axis=1, tiled=True)  16.9 us
    dot_general x1, matrix products, patch_heads(): jnp.einsum('hqk,khd->qhd', weights, value_heads, preferred_element_type=j...  14.3 us
  transfers between devices with their start and end apart: 8, of which 7 were waited for; matrix products, arithmetic and copies ran while one was open for 4% of the time, Pallas kernels for 0%

commit v1 on v0

v1 whole, which is shorter than its diff:
```python
import functools

import jax
import jax.numpy as jnp
from jax import lax
from jax.experimental import pallas as pl
from jax.experimental.pallas import tpu as pltpu
from jax.sharding import PartitionSpec as P

HD = 64
PATCH = 256
REACH = 2
LANES = 128
VMEM_LIMIT = 58 * 1024 * 1024

epsilon = 1e-06
OFFSETS = [stride for stride in range(1, REACH + 1)] + [-stride for stride in range(1, REACH + 1)]


def passed_along(value, axis, steps):
    count = lax.axis_size(axis)
    pairs = [(source, (source + steps) % count) for source in range(count)]
    return lax.ppermute(value, axis, pairs)


def normalized(widened, scaling):
    mean_square = jnp.mean(widened * widened, axis=-1, keepdims=True)
    return (widened * lax.rsqrt(mean_square + epsilon) * scaling).astype(jnp.bfloat16)


def project(inputs, weight):
    return jnp.dot(inputs, weight, preferred_element_type=jnp.float32).astype(jnp.bfloat16)


def vertical_kernel(x_ref, gain_ref, wq_ref, wk_ref, wv_ref, wo_ref, bias_ref, hidden_ref, attn_ref):
    levels, columns, features = x_ref.shape
    tokens = levels * columns
    x = x_ref[...].reshape(tokens, features).astype(jnp.float32)
    normed = normalized(x, gain_ref[...])
    queries = project(normed, wq_ref[...]).astype(jnp.float32)
    keys = project(normed, wk_ref[...]).astype(jnp.float32)
    values = project(normed, wv_ref[...]).astype(jnp.float32)
    head_of = lax.broadcasted_iota(jnp.int32, (features, LANES), 0) // HD
    gather_heads = (head_of == lax.broadcasted_iota(jnp.int32, (features, LANES), 1)).astype(jnp.bfloat16)
    head_to = lax.broadcasted_iota(jnp.int32, (LANES, features), 1) // HD
    spread_heads = (head_to == lax.broadcasted_iota(jnp.int32, (LANES, features), 0)).astype(jnp.bfloat16)
    for i in range(levels):
        query = queries[i * columns : (i + 1) * columns]
        products = jnp.concatenate(
            [(query * keys[j * columns : (j + 1) * columns]).astype(jnp.bfloat16) for j in range(levels)], axis=0
        )
        summed = jnp.dot(products, gather_heads, preferred_element_type=jnp.float32) * HD ** (-0.5)
        scores = [
            summed[j * columns : (j + 1) * columns] + bias_ref[i * levels + j : i * levels + j + 1, :]
            for j in range(levels)
        ]
        top = functools.reduce(jnp.maximum, scores)
        raised = [jnp.exp(score - top) for score in scores]
        inverse = 1.0 / functools.reduce(jnp.add, raised)
        weights = jnp.concatenate([(each * inverse).astype(jnp.bfloat16) for each in raised], axis=0)
        spread = jnp.dot(weights, spread_heads, preferred_element_type=jnp.float32)
        mixed = functools.reduce(
            jnp.add,
            [
                spread[j * columns : (j + 1) * columns] * values[j * columns : (j + 1) * columns]
                for j in range(levels)
            ],
        )
        attn_ref[i * columns : (i + 1) * columns, :] = mixed.astype(jnp.bfloat16)
    hidden = x + jnp.dot(attn_ref[...], wo_ref[...], preferred_element_type=jnp.float32)
    hidden_ref[...] = hidden.astype(jnp.bfloat16).reshape(levels, columns, features)


def vertical(merged, gain, wq, wk, wv, wo, bias_rows):
    levels, columns, features = merged.shape
    vmem = pl.BlockSpec(memory_space=pltpu.VMEM)
    return pl.pallas_call(
        vertical_kernel,
        out_shape=jax.ShapeDtypeStruct(merged.shape, jnp.bfloat16),
        in_specs=[vmem] * 7,
        out_specs=vmem,
        scratch_shapes=[pltpu.VMEM((levels * columns, features), jnp.bfloat16)],
        compiler_params=pltpu.CompilerParams(vmem_limit_bytes=VMEM_LIMIT),
        name="vertical",
    )(merged, gain, wq, wk, wv, wo, bias_rows)


def choices(nb_ref, count_ref, patch, offset, cycle, per_device):
    source = lax.rem(lax.axis_index("space") + cycle - offset, cycle)
    live = jnp.int32(0)
    within = jnp.int32(0)
    for m in range(nb_ref.shape[1]):
        listed = jnp.maximum(nb_ref[patch, m], 0)
        hit = jnp.logical_and(m < count_ref[patch], lax.div(listed, per_device) == source)
        live = jnp.where(hit, 1, live)
        within = jnp.where(hit, lax.rem(listed, per_device), within)
    return live, within


def attend(q_ref, k_ref, v_ref, attn_ref, pb_ref, nb_ref, count_ref, cycle):
    tokens, features = q_ref.shape
    per_device = tokens // PATCH
    far = len(OFFSETS) * per_device
    low = lax.broadcasted_iota(jnp.int32, (1, LANES), 1) < HD
    for patch in range(per_device):
        rows = pl.ds(patch * PATCH, PATCH)
        picked = [choices(nb_ref, count_ref, patch, offset, cycle, per_device) for offset in OFFSETS]
        blocks = [far + patch] + [o * per_device + within for o, (_, within) in enumerate(picked)]

        def pair(step, carry):
            lanes = pl.ds(pl.multiple_of(step * LANES, LANES), LANES)
            query = q_ref[rows, lanes]
            results = []
            for parity in range(2):
                head = step * 2 + parity
                mine = low if parity == 0 else jnp.logical_not(low)
                masked = jnp.where(mine, query, jnp.zeros_like(query))
                scores = [
                    lax.dot_general(
                        masked, k_ref[block, :, lanes], (((1,), (1,)), ((), ())), preferred_element_type=jnp.float32
                    )
                    for block in blocks
                ]
                adds = [pb_ref[head, 0]] + [
                    jnp.where(live > 0, pb_ref[head, 1], jnp.float32(-1e30)) for live, _ in picked
                ]
                top = functools.reduce(
                    jnp.maximum, [jnp.max(s, axis=-1, keepdims=True) + a for s, a in zip(scores, adds)]
                )
                raised = [jnp.exp(s + (a - top)) for s, a in zip(scores, adds)]
                total = functools.reduce(jnp.add, [jnp.sum(r, axis=-1, keepdims=True) for r in raised])
                mixed = functools.reduce(
                    jnp.add,
                    [
                        jnp.dot(r.astype(jnp.bfloat16), v_ref[block, :, lanes], preferred_element_type=jnp.float32)
                        for r, block in zip(raised, blocks)
                    ],
                )
                results.append(mixed / total)
            attn_ref[rows, lanes] = jnp.where(low, results[0], results[1]).astype(jnp.bfloat16)
            return carry

        lax.fori_loop(0, features // LANES, pair, 0)


def patch_kernel(cycle, xo_ref, xf_ref, hid_ref, cot_ref, wq_ref, wk_ref, wv_ref, wo_ref, pb_ref, nb_ref, count_ref,
                 out_ref, grad_ref, q_ref, k_ref, v_ref, attn_ref):
    tokens, features = xo_ref.shape
    per_device = tokens // PATCH
    far = len(OFFSETS) * per_device
    own = xo_ref[...]
    q_ref[...] = (jnp.dot(own, wq_ref[...], preferred_element_type=jnp.float32).astype(jnp.bfloat16)
                  * jnp.bfloat16(HD ** (-0.5)))
    k_ref[far:] = project(own, wk_ref[...]).reshape(per_device, PATCH, features)
    v_ref[far:] = project(own, wv_ref[...]).reshape(per_device, PATCH, features)

    def distant(step, carry):
        block = xf_ref[step]
        k_ref[step] = project(block, wk_ref[...])
        v_ref[step] = project(block, wv_ref[...])
        return carry

    lax.fori_loop(0, far, distant, 0)
    attend(q_ref, k_ref, v_ref, attn_ref, pb_ref, nb_ref, count_ref, cycle)
    attn = attn_ref[...]
    grad_ref[...] = lax.dot_general(
        attn, cot_ref[...], (((0,), (0,)), ((), ())), preferred_element_type=jnp.float32
    ).astype(jnp.bfloat16)
    out_ref[...] = (
        hid_ref[...].astype(jnp.float32) + jnp.dot(attn, wo_ref[...], preferred_element_type=jnp.float32)
    ).astype(jnp.bfloat16)


def patch_stage(xo, xf, hidden, cot, wq, wk, wv, wo, pb, nb, counts):
    tokens, features = xo.shape
    blocks = (len(OFFSETS) + 1) * (tokens // PATCH)
    vmem = pl.BlockSpec(memory_space=pltpu.VMEM)
    smem = pl.BlockSpec(memory_space=pltpu.SMEM)
    return pl.pallas_call(
        functools.partial(patch_kernel, lax.axis_size("space")),
        out_shape=(
            jax.ShapeDtypeStruct((tokens, features), jnp.bfloat16),
            jax.ShapeDtypeStruct((features, features), jnp.bfloat16),
        ),
        in_specs=[vmem] * 8 + [smem] * 3,
        out_specs=(vmem, vmem),
        scratch_shapes=[
            pltpu.VMEM((tokens, features), jnp.bfloat16),
            pltpu.VMEM((blocks, PATCH, features), jnp.bfloat16),
            pltpu.VMEM((blocks, PATCH, features), jnp.bfloat16),
            pltpu.VMEM((tokens, features), jnp.bfloat16),
        ],
        compiler_params=pltpu.CompilerParams(vmem_limit_bytes=VMEM_LIMIT),
        name="patch_stage",
    )(xo, xf, hidden, cot, wq, wk, wv, wo, pb, nb, counts)


def body(fields, norm_vert, query_vert, keys_vert, values_vert, out_vert, level_bias, norm_patch, query_patch,
         keys_patch, values_patch, out_patch, patch_bias, neighbours, counts, cotangent):
    _, columns, features = fields.shape
    groups = lax.axis_size("level")
    heads = level_bias.shape[0]
    bias_rows = jnp.pad(
        jnp.transpose(level_bias, (1, 2, 0)).reshape(groups * groups, heads), ((0, 0), (0, LANES - heads))
    )
    split = fields.reshape(groups, columns // groups, features)
    merged = lax.all_to_all(split, "level", split_axis=0, concat_axis=0, tiled=True)
    mixed = vertical(merged, norm_vert[None], query_vert, keys_vert, values_vert, out_vert, bias_rows)
    hidden = lax.all_to_all(mixed, "level", split_axis=0, concat_axis=0, tiled=True).reshape(columns, features)
    normed = normalized(hidden.astype(jnp.float32), norm_patch)
    arrived = jnp.concatenate([passed_along(normed, "space", offset)[None] for offset in OFFSETS])
    out, grad = patch_stage(normed, arrived.reshape(-1, PATCH, features), hidden, cotangent[0], query_patch,
                            keys_patch, values_patch, out_patch, patch_bias, neighbours, counts)
    shares = lax.psum_scatter(grad, "space", scatter_dimension=0, tiled=True)
    grad_wo = lax.psum(shares, "level").astype(jnp.float32)
    return (out[None], grad_wo)


def solution(mesh):
    split = P("level", "space", None)
    return jax.shard_map(
        body,
        mesh=mesh,
        in_specs=(split,) + (P(),) * 12 + (P("space", None), P("space"), split),
        out_specs=(split, P("space", None)),
        check_vma=False,
    )
```

time: 336 us -> 236 us (0.70)
  matrix products: 70.3 us -> 0 us
  local copies, waits for them, and re-layouts: 46.4 us -> 2.78 us
  waiting for transfers between devices: 180 us -> 140 us
  Pallas kernels: 0 us -> 39.6 us
  blocking collectives: 0 us -> 23.3 us
  other arithmetic: 10.9 us -> 5.07 us
    all_to_all x2 -> x1, waiting for transfers between devices: 70 us -> 18.9 us  [body(): lax.all_to_all(split, 'level', split_axis=0, concat_axis=0, tiled=True)]
    dot_general x9 -> x0, matrix products: 43.9 us -> none  [the longest x4 18.6 us: project(): jnp.dot(inputs, weight, preferred_element_type=jnp.float32)]
    pallas_call x0 -> x2, Pallas kernels: none -> 39.6 us  [the longest x1 31.4 us: patch_stage(): pl.pallas_call(functools.partial(patch_kernel, lax.axis_size('space')), o...]
    sub x2 -> x0, matrix products: 26.4 us -> none  [the longest x1 17.4 us: patch_heads(): weights = jax.nn.softmax(scores, axis=-1).astype(jnp.bfloat16)]
    all_to_all x0 -> x1, blocking collectives: none -> 23.3 us  [body(): lax.all_to_all(mixed, 'level', split_axis=0, concat_axis=0, tiled=True)]
    slice x6 -> x0, local copies, waits for them, and re-layouts: 19.7 us -> none  [the longest x2 11.7 us: patch_heads(): key_heads = keys_all[:, :features].reshape(-1, H, HD)]
    reshape x4 -> x0, local copies, waits for them, and re-layouts: 10.7 us -> none  [the longest x1 3.56 us: vertical_heads(): key_heads = keys_in.reshape(keys_in.shape[0], columns, H, HD)]
    ppermute x4, waiting for transfers between devices: 42.3 us -> 49.5 us  [passed_along(): return lax.ppermute(value, axis, pairs)]
  transfers between devices with their start and end apart: 8 -> 7, of which waited for: 7 -> 7; matrix products, arithmetic and copies ran while one was open for 4% -> 1% of each run, Pallas kernels for 0% -> 0%
where the time goes in v1:
time: 236 us
  waiting for transfers between devices  140 us (59%)
  Pallas kernels  39.6 us (17%)
  blocking collectives  23.3 us (10%)
  between operations  14.1 us (6%)
  starting transfers between devices  11 us (5%)
  other arithmetic  5.07 us (2%)
  local copies, waits for them, and re-layouts  2.78 us (1%)
    ppermute x4, waiting for transfers between devices, passed_along(): return lax.ppermute(value, axis, pairs)  49.5 us
    psum x1, waiting for transfers between devices, body(): grad_wo = lax.psum(shares, 'level').astype(jnp.float32)  36.8 us
    reduce_scatter x1, waiting for transfers between devices, body(): shares = lax.psum_scatter(grad, 'space', scatter_dimension=0, tiled=True)  34.9 us
    pallas_call x1, Pallas kernels, patch_stage(): pl.pallas_call(functools.partial(patch_kernel, lax.axis_size('space')), o...  31.4 us
    all_to_all x1, blocking collectives, body(): lax.all_to_all(mixed, 'level', split_axis=0, concat_axis=0, tiled=True)  23.3 us
    all_to_all x1, waiting for transfers between devices, body(): lax.all_to_all(split, 'level', split_axis=0, concat_axis=0, tiled=True)  18.9 us
    pallas_call x1, Pallas kernels, vertical(): pl.pallas_call(vertical_kernel, out_shape=jax.ShapeDtypeStruct(merged.sha...  8.24 us
    all_to_all x1, starting transfers between devices, body(): lax.all_to_all(split, 'level', split_axis=0, concat_axis=0, tiled=True)  6.49 us
  transfers between devices with their start and end apart: 7, of which 7 were waited for; matrix products, arithmetic and copies ran while one was open for 1% of the time, Pallas kernels for 0%

profile of v1, /device:TPU:0, one launch (start us, length us, event | category | flops | bytes accessed | tf_op | source)
XLA Modules:
  0.0 236.0 jit_solution(12962513200113271808)
XLA Ops:
  7.2 0.0 copy-start.5
  7.2 0.0 copy-start.3
  7.2 6.5 %all-to-all-start = ((bf16[4,128,768]{2,1,0:T(8,128)(2,1)}), bf16[4,128,768]{2,1,0:T(8,128)(2,1)S(1)}, u32[]{:S(2)}, u32[]{:S(2)}) async-start(bf16[4,128,768]{2,1,0:T(8,128)(2,1)} %bitcast.20), calls=%async_computation | async-start | bytes 1572864 | tf_op jit(solution)/shard_map/all_to_all | solution.py:207
  13.7 0.0 reduce-scatter.2.cloned.1.call-start
  13.7 0.0 copy-done.5
  13.7 0.6 broadcast_in_dim.20.gain_ref
  14.3 0.0 copy-done.3
  14.3 0.6 pad.4.bias_ref
  14.9 18.9 %all-to-all-done.x_ref = bf16[4,128,768]{2,1,0:T(8,128)(2,1)S(1)} async-done(((bf16[4,128,768]{2,1,0:T(8,128)(2,1)}), bf16[4,128,768]{2,1,0:T(8,128)(2,1)S(1)}, u32[]{:S(2)}, u32[]{:S(2)}) %all-to-all-start) | async-done | bytes 786464 | tf_op jit(solution)/shard_map/all_to_all | solution.py:207
  33.8 0.0 copy-start.2
  33.8 0.9 copy-done.2
  34.7 8.2 %vertical.1 = bf16[4,128,768]{2,1,0:T(8,128)(2,1)} custom-call(bf16[4,128,768]{2,1,0:T(8,128)(2,1)} %copy-done.2, f32[1,768]{1,0:T(1,128)} %broadcast_in_dim.20.gain_ref, bf16[768,768]{1,0:T(8,128)(2,1)} %wq_ref.2, bf16[768,768]{1,0:T(8,128)(2,1)} %wk_ref.2, bf16[768,768]{1,0:T(8,128)(2,1)} %wv_ref.2, bf16[768,768]{1,0:T(8,128)(2,1)} %wo_ref.2, ...), custom_call_target="tpu_custom_call" | custom-call | tf_op jit(solution)/shard_map/vertical/pallas_call | solution.py:77
  42.9 0.0 copy-start.4
  42.9 23.3 %all_to_all.10 = bf16[4,128,768]{2,1,0:T(8,128)(2,1)S(1)} all-to-all(bf16[4,128,768]{2,1,0:T(8,128)(2,1)} %vertical.1), channel_id=1, replica_groups=mesh['space'=8,'level'=4] {'level'}, dimensions={0} | all-to-all | bytes 1572864 | tf_op jit(solution)/shard_map/all_to_all | solution.py:209
  66.2 0.0 copy-start
  66.2 0.0 copy-start.6
  66.2 0.2 multiply_reduce_fusion
  66.4 0.0 copy-done.4
  66.4 0.2 multiply_convert_fusion.xo_ref
  66.7 0.0 copy-start.1
  66.7 0.1 collective-permute-start
  66.8 1.5 collective-permute-start.1
  68.3 2.3 collective-permute-start.2
  70.6 0.5 collective-permute-start.3
  71.1 0.0 copy-done.6
  71.1 0.7 copy.18.pb_ref
  71.8 15.0 %collective-permute-done = bf16[512,768]{1,0:T(8,128)(2,1)S(1)} collective-permute-done((bf16[512,768]{1,0:T(8,128)(2,1)S(1)}, bf16[512,768]{1,0:T(8,128)(2,1)S(1)}, u32[]{:S(2)}, u32[]{:S(2)}) %collective-permute-start) | collective-permute-done | bytes 786464 | tf_op jit(solution)/shard_map/ppermute | solution.py:23
  86.8 1.3 collective-permute-done.1
  88.1 15.0 %collective-permute-done.2 = bf16[512,768]{1,0:T(8,128)(2,1)} collective-permute-done((bf16[512,768]{1,0:T(8,128)(2,1)S(1)}, bf16[512,768]{1,0:T(8,128)(2,1)}, u32[]{:S(2)}, u32[]{:S(2)}) %collective-permute-start.2) | collective-permute-done | bytes 786464 | tf_op jit(solution)/shard_map/ppermute | solution.py:23
  103.1 18.3 %collective-permute-done.3 = bf16[512,768]{1,0:T(8,128)(2,1)} collective-permute-done((bf16[512,768]{1,0:T(8,128)(2,1)S(1)}, bf16[512,768]{1,0:T(8,128)(2,1)}, u32[]{:S(2)}, u32[]{:S(2)}) %collective-permute-start.3) | collective-permute-done | bytes 786464 | tf_op jit(solution)/shard_map/ppermute | solution.py:23
  121.3 2.9 %pad_maximum_fusion = bf16[4,512,768]{2,1,0:T(8,128)(2,1)} fusion(bf16[1,512,768]{2,1,0:T(8,128)(2,1)} %bitcast.8, bf16[1,512,768]{2,1,0:T(8,128)(2,1)} %bitcast.7, bf16[1,512,768]{2,1,0:T(8,128)(2,1)S(1)} %bitcast.19, bf16[1,512,768]{2,1,0:T(8,128)(2,1)S(1)} %bitcast.18), kind=kLoop, calls=%fused_computation | loop fusion | flops 4718592 | bytes 6291456 | tf_op jit(solution)/shard_map/concatenate | solution.py:211
  124.3 0.0 copy-done
  124.3 0.0 copy-done.1
  124.3 31.4 %patch_stage.1 = (bf16[512,768]{1,0:T(8,128)(2,1)}, bf16[768,768]{1,0:T(8,128)(2,1)}) custom-call(bf16[512,768]{1,0:T(8,128)(2,1)} %copy-done.1, bf16[8,256,768]{2,1,0:T(8,128)(2,1)} %bitcast.16, bf16[512,768]{1,0:T(8,128)(2,1)} %bitcast.15, bf16[512,768]{1,0:T(8,128)(2,1)} %bitcast.17, bf16[768,768]{1,0:T(8,128)(2,1)} %wq_ref.3, bf16[768,768]{1,0:T(8,128)(2,1)} %wk_ref.3, ...), custom_call_target="tpu_custom_call" | custom-call | tf_op jit(solution)/shard_map/patch_stage/pallas_call | solution.py:179
  155.7 0.0 reduce-scatter.2.cloned.1.call-update
  155.7 0.0 all-reduce.3.cloned.1.call-start
  155.8 34.9 %reduce-scatter.2.cloned.1.call-done = bf16[96,768]{1,0:T(8,128)(2,1)} async-done(((bf16[768,768]{1,0:T(8,128)(2,1)}), bf16[96,768]{1,0:T(8,128)(2,1)}) %reduce-scatter.2.cloned.1.call-update) | async-done | bytes 147472 | tf_op jit(solution)/shard_map/reduce_scatter | solution.py:214
  190.7 0.0 all-reduce.3.cloned.1.call-update
  190.7 36.8 %all-reduce.3.cloned.1.call-done = bf16[96,768]{1,0:T(8,128)(2,1)} async-done(((bf16[96,768]{1,0:T(8,128)(2,1)}), bf16[96,768]{1,0:T(8,128)(2,1)}) %all-reduce.3.cloned.1.call-update) | async-done | bytes 147472 | tf_op jit(solution)/shard_map/psum | solution.py:215
  227.5 1.6 convert_element_type.17
  (1 shorter events, 0.0 us)
Async XLA Ops:
  7.2 6.5 %copy-start.5 = (f32[768]{0:T(1024)S(1)}, f32[768]{0:T(1024)}, u32[]{:S(2)}) copy-start(f32[768]{0:T(1024)} %param.17) | copy-start | bytes 9220
  7.2 7.1 %copy-start.3 = (f32[12,4,4]{0,2,1:T(4,128)S(1)}, f32[12,4,4]{0,2,1:T(4,128)}, u32[]{:S(2)}) copy-start(f32[12,4,4]{0,2,1:T(4,128)} %param.22) | copy-start | bytes 2308
  7.2 26.6 %all-to-all-start = ((bf16[4,128,768]{2,1,0:T(8,128)(2,1)}), bf16[4,128,768]{2,1,0:T(8,128)(2,1)S(1)}, u32[]{:S(2)}, u32[]{:S(2)}) async-start(bf16[4,128,768]{2,1,0:T(8,128)(2,1)} %bitcast.20), calls=%async_computation | async-start | bytes 1572864 | tf_op jit(solution)/shard_map/all_to_all | solution.py:207
  13.7 177.0 %reduce-scatter.2.cloned.1.call-start = ((), (), s32[]{:S(2)}) async-start(), calls=%async_computation.3 | async-start | bytes 1327104 | tf_op jit(solution)/shard_map/reduce_scatter | solution.py:214
  33.8 0.9 copy-start.2
  42.9 23.5 %copy-start.4 = (f32[768]{0:T(1024)S(1)}, f32[768]{0:T(1024)}, u32[]{:S(2)}) copy-start(f32[768]{0:T(1024)} %param.23) | copy-start | bytes 9220
  66.2 58.1 %copy-start = (bf16[4,128,768]{2,1,0:T(8,128)(2,1)}, bf16[4,128,768]{2,1,0:T(8,128)(2,1)S(1)}, u32[]{:S(2)}) copy-start(bf16[4,128,768]{2,1,0:T(8,128)(2,1)S(1)} %all_to_all.10) | copy-start | bytes 2359300
  66.2 5.0 %copy-start.6 = (f32[12,2]{0,1:T(2,128)S(1)}, f32[12,2]{0,1:T(2,128)}, u32[]{:S(2)}) copy-start(f32[12,2]{0,1:T(2,128)} %param.28) | copy-start | bytes 292
  66.7 57.6 %copy-start.1 = (bf16[512,768]{1,0:T(8,128)(2,1)}, bf16[512,768]{1,0:T(8,128)(2,1)S(1)}, u32[]{:S(2)}) copy-start(bf16[512,768]{1,0:T(8,128)(2,1)S(1)} %multiply_convert_fusion.xo_ref) | copy-start | bytes 2359300
  66.7 20.2 %collective-permute-start = (bf16[512,768]{1,0:T(8,128)(2,1)S(1)}, bf16[512,768]{1,0:T(8,128)(2,1)S(1)}, u32[]{:S(2)}, u32[]{:S(2)}) collective-permute-start(bf16[512,768]{1,0:T(8,128)(2,1)S(1)} %multiply_convert_fusion.xo_ref), channel_id=1, source_target_pairs={{0,4},{4,8},{8,12},{12,16},{16,20},{20,24},{24,28},{28,0},{1,5},{5... | collective-permute-start | bytes 2359304 | tf_op jit(solution)/shard_map/ppermute | solution.py:23
  66.8 21.4 %collective-permute-start.1 = (bf16[512,768]{1,0:T(8,128)(2,1)S(1)}, bf16[512,768]{1,0:T(8,128)(2,1)S(1)}, u32[]{:S(2)}, u32[]{:S(2)}) collective-permute-start(bf16[512,768]{1,0:T(8,128)(2,1)S(1)} %multiply_convert_fusion.xo_ref), channel_id=1, source_target_pairs={{0,8},{4,12},{8,16},{12,20},{16,24},{20,28},{24,0},{28,4},{1,9},{5... | collective-permute-start | bytes 2359304 | tf_op jit(solution)/shard_map/ppermute | solution.py:23
  68.3 34.8 %collective-permute-start.2 = (bf16[512,768]{1,0:T(8,128)(2,1)S(1)}, bf16[512,768]{1,0:T(8,128)(2,1)}, u32[]{:S(2)}, u32[]{:S(2)}) collective-permute-start(bf16[512,768]{1,0:T(8,128)(2,1)S(1)} %multiply_convert_fusion.xo_ref), channel_id=1, source_target_pairs={{0,28},{4,0},{8,4},{12,8},{16,12},{20,16},{24,20},{28,24},{1,29},{... | collective-permute-start | bytes 2359304 | tf_op jit(solution)/shard_map/ppermute | solution.py:23
  70.6 50.8 %collective-permute-start.3 = (bf16[512,768]{1,0:T(8,128)(2,1)S(1)}, bf16[512,768]{1,0:T(8,128)(2,1)}, u32[]{:S(2)}, u32[]{:S(2)}) collective-permute-start(bf16[512,768]{1,0:T(8,128)(2,1)S(1)} %multiply_convert_fusion.xo_ref), channel_id=1, source_target_pairs={{0,24},{4,28},{8,0},{12,4},{16,8},{20,12},{24,16},{28,20},{1,25},{... | collective-permute-start | bytes 2359304 | tf_op jit(solution)/shard_map/ppermute | solution.py:23
  155.7 71.8 %all-reduce.3.cloned.1.call-start = ((), (), s32[]{:S(2)}) async-start(), calls=%async_computation.4 | async-start | bytes 294912 | tf_op jit(solution)/shard_map/psum | solution.py:215
Sparse Core Ops, SparseCore 0:
  155.8 34.8 reduce-scatter.1
  193.0 34.4 all-reduce.2

commit v2 on v1

v2 whole, which is shorter than its diff:
```python
import functools

import jax
import jax.numpy as jnp
from jax import lax
from jax.experimental import pallas as pl
from jax.experimental.pallas import tpu as pltpu
from jax.sharding import PartitionSpec as P

HD = 64
PATCH = 256
LANES = 128
VMEM_LIMIT = 58 * 1024 * 1024

epsilon = 1e-06


def normalized(widened, scaling):
    mean_square = jnp.mean(widened * widened, axis=-1, keepdims=True)
    return (widened * lax.rsqrt(mean_square + epsilon) * scaling).astype(jnp.bfloat16)


def project(inputs, weight):
    return jnp.dot(inputs, weight, preferred_element_type=jnp.float32).astype(jnp.bfloat16)


def vertical(x, gain, wq, wk, wv, wo, bias_rows, attn_ref):
    levels, columns, features = x.shape
    tokens = levels * columns
    x = x.reshape(tokens, features).astype(jnp.float32)
    normed = normalized(x, gain)
    queries = project(normed, wq).astype(jnp.float32)
    keys = project(normed, wk).astype(jnp.float32)
    values = project(normed, wv).astype(jnp.float32)
    head_of = lax.broadcasted_iota(jnp.int32, (features, LANES), 0) // HD
    gather_heads = (head_of == lax.broadcasted_iota(jnp.int32, (features, LANES), 1)).astype(jnp.bfloat16)
    head_to = lax.broadcasted_iota(jnp.int32, (LANES, features), 1) // HD
    spread_heads = (head_to == lax.broadcasted_iota(jnp.int32, (LANES, features), 0)).astype(jnp.bfloat16)
    for i in range(levels):
        query = queries[i * columns : (i + 1) * columns]
        products = jnp.concatenate(
            [(query * keys[j * columns : (j + 1) * columns]).astype(jnp.bfloat16) for j in range(levels)], axis=0
        )
        summed = jnp.dot(products, gather_heads, preferred_element_type=jnp.float32) * HD ** (-0.5)
        scores = [
            summed[j * columns : (j + 1) * columns] + bias_rows[i * levels + j]
            for j in range(levels)
        ]
        top = functools.reduce(jnp.maximum, scores)
        raised = [jnp.exp(score - top) for score in scores]
        inverse = 1.0 / functools.reduce(jnp.add, raised)
        weights = jnp.concatenate([(each * inverse).astype(jnp.bfloat16) for each in raised], axis=0)
        spread = jnp.dot(weights, spread_heads, preferred_element_type=jnp.float32)
        mixed = functools.reduce(
            jnp.add,
            [
                spread[j * columns : (j + 1) * columns] * values[j * columns : (j + 1) * columns]
                for j in range(levels)
            ],
        )
        attn_ref[i * columns : (i + 1) * columns, :] = mixed.astype(jnp.bfloat16)
    hidden = x + jnp.dot(attn_ref[...], wo, preferred_element_type=jnp.float32)
    return hidden.astype(jnp.bfloat16).reshape(levels, columns, features)


def choices(nb_ref, count_ref, patch, source, per_device):
    live = jnp.int32(0)
    within = jnp.int32(0)
    for m in range(nb_ref.shape[1]):
        listed = jnp.maximum(nb_ref[patch, m], 0)
        hit = jnp.logical_and(m < count_ref[patch], lax.div(listed, per_device) == source)
        live = jnp.where(hit, 1, live)
        within = jnp.where(hit, lax.rem(listed, per_device), within)
    return live, within


def attend(q_ref, k_ref, v_ref, attn_ref, pb_ref, nb_ref, count_ref, sources):
    tokens, features = q_ref.shape
    per_device = tokens // PATCH
    far = len(sources) * per_device
    low = lax.broadcasted_iota(jnp.int32, (1, LANES), 1) < HD
    for patch in range(per_device):
        rows = pl.ds(patch * PATCH, PATCH)
        picked = [choices(nb_ref, count_ref, patch, source, per_device) for source in sources]
        blocks = [far + patch] + [o * per_device + within for o, (_, within) in enumerate(picked)]

        def pair(step, carry):
            lanes = pl.ds(pl.multiple_of(step * LANES, LANES), LANES)
            query = q_ref[rows, lanes]
            results = []
            for parity in range(2):
                head = step * 2 + parity
                mine = low if parity == 0 else jnp.logical_not(low)
                masked = jnp.where(mine, query, jnp.zeros_like(query))
                scores = [
                    lax.dot_general(
                        masked, k_ref[block, :, lanes], (((1,), (1,)), ((), ())), preferred_element_type=jnp.float32
                    )
                    for block in blocks
                ]
                adds = [pb_ref[head, 0]] + [
                    jnp.where(live > 0, pb_ref[head, 1], jnp.float32(-1e30)) for live, _ in picked
                ]
                top = functools.reduce(
                    jnp.maximum, [jnp.max(s, axis=-1, keepdims=True) + a for s, a in zip(scores, adds)]
                )
                raised = [jnp.exp(s + (a - top)) for s, a in zip(scores, adds)]
                total = functools.reduce(jnp.add, [jnp.sum(r, axis=-1, keepdims=True) for r in raised])
                mixed = functools.reduce(
                    jnp.add,
                    [
                        jnp.dot(r.astype(jnp.bfloat16), v_ref[block, :, lanes], preferred_element_type=jnp.float32)
                        for r, block in zip(raised, blocks)
                    ],
                )
                results.append(mixed / total)
            attn_ref[rows, lanes] = jnp.where(low, results[0], results[1]).astype(jnp.bfloat16)
            return carry

        lax.fori_loop(0, features // LANES, pair, 0)


def remote(src, dst, send, recv, device):
    return pltpu.make_async_remote_copy(
        src_ref=src, dst_ref=dst, send_sem=send, recv_sem=recv, device_id=device,
        device_id_type=pl.DeviceIdType.MESH,
    )


def whole_kernel(cycle, levels, x_ref, nv_ref, np_ref, wqv_hbm, wkv_hbm, wvv_hbm, wov_hbm, wqp_hbm, wkp_hbm, wvp_hbm,
                 wop_hbm, cot_hbm, lb_ref, pb_ref, nb_ref, count_ref, out_ref, grad_ref, weight_ref, cot_ref, in_ref,
                 hsend_ref, hid_ref, attn_ref, own_ref, far_ref, q_ref, k_ref, v_ref, gsend_ref, grecv_ref, lsend_ref,
                 lrecv_ref, final_ref, load_sem, in_send, in_recv, back_send, back_recv, halo_send, halo_recv,
                 share_send, share_recv, part_send, part_recv, full_send, full_recv):
    chunks, _, columns, features = x_ref.shape
    place = lax.axis_index("space")
    level = lax.axis_index("level")
    weights_hbm = (wqv_hbm, wkv_hbm, wvv_hbm, wov_hbm, wqp_hbm, wkp_hbm, wvp_hbm, wop_hbm)
    loads = [pltpu.make_async_copy(w, weight_ref.at[i], load_sem.at[i]) for i, w in enumerate(weights_hbm)]
    loads.append(pltpu.make_async_copy(cot_hbm, cot_ref, load_sem.at[len(weights_hbm)]))
    for load in loads:
        load.start()

    barrier = pltpu.get_barrier_semaphore()
    peers = [lax.rem(level + k, levels) for k in range(1, levels)]
    around = [lax.rem(place + k, cycle) for k in range(1, cycle)]
    for peer in peers:
        pl.semaphore_signal(barrier, inc=1, device_id={"level": peer}, device_id_type=pl.DeviceIdType.MESH)
    for peer in around:
        pl.semaphore_signal(barrier, inc=1, device_id={"space": peer}, device_id_type=pl.DeviceIdType.MESH)
    pl.semaphore_wait(barrier, levels - 1 + cycle - 1)

    inward = []
    for c in range(chunks):
        steps = []
        for k, peer in enumerate(peers):
            steps.append(remote(x_ref.at[c, peer], in_ref.at[c, level], in_send.at[c, k], in_recv.at[c, k],
                                {"level": peer}))
            steps[-1].start()
        in_ref[c, level] = x_ref[c, level]
        inward.append(steps)

    lane = lax.broadcasted_iota(jnp.int32, (1, LANES), 1)
    bias_rows = []
    for i in range(levels):
        for j in range(levels):
            row = jnp.zeros((1, LANES), jnp.float32)
            for h in range(lb_ref.shape[0]):
                row = jnp.where(lane == h, lb_ref[h, i, j], row)
            bias_rows.append(row)
    for load in loads[:4]:
        load.wait()

    back = []
    for c in range(chunks):
        for step in inward[c]:
            step.wait_recv()
        hsend_ref[c] = vertical(in_ref[c], nv_ref[...], weight_ref[0], weight_ref[1], weight_ref[2], weight_ref[3],
                                bias_rows, attn_ref.at[pl.ds(0, PATCH)])
        steps = []
        for k, peer in enumerate(peers):
            steps.append(remote(hsend_ref.at[c, peer], hid_ref.at[c, level], back_send.at[c, k], back_recv.at[c, k],
                                {"level": peer}))
            steps[-1].start()
        hid_ref[c, level] = hsend_ref[c, level]
        back.append(steps)
    for load in loads[4:]:
        load.wait()

    toward = lax.rem(place, 2) * 2 - 1
    sources = [lax.rem(place + step * toward + 2 * cycle, cycle) for step in (1, 2, -1, -2)]
    partner = sources[2]
    far = len(sources) * chunks
    scale = jnp.bfloat16(HD ** (-0.5))
    halo = []
    for c in range(chunks):
        for step in back[c]:
            step.wait_recv()
        normed = normalized(hid_ref[c].reshape(levels * columns, features).astype(jnp.float32), np_ref[...])
        own_ref[c] = normed
        steps = []
        for slot, target in ((0, sources[0]), (1, sources[3]), (2, partner)):
            steps.append(remote(own_ref.at[c], far_ref.at[slot * chunks + c], halo_send.at[c, slot],
                                halo_recv.at[c, slot], {"space": target}))
            steps[-1].start()
        halo.append(steps)
        q_ref[pl.ds(c * PATCH, PATCH), :] = project(normed, weight_ref[4]) * scale
        k_ref[far + c] = project(normed, weight_ref[5])
        v_ref[far + c] = project(normed, weight_ref[6])
    def distant(block):
        k_ref[block] = project(far_ref[block], weight_ref[5])
        v_ref[block] = project(far_ref[block], weight_ref[6])

    for c in range(chunks):
        halo[c][2].wait_recv()
        distant(2 * chunks + c)
        halo[c][0].wait_recv()
        passed = remote(far_ref.at[c], far_ref.at[3 * chunks + c], halo_send.at[c, 3], halo_recv.at[c, 3],
                        {"space": partner})
        passed.start()
        halo[c].append(passed)
        distant(c)
        halo[c][1].wait_recv()
        distant(chunks + c)
    for c in range(chunks):
        halo[c][3].wait_recv()
        distant(3 * chunks + c)

    attend(q_ref, k_ref, v_ref, attn_ref, pb_ref, nb_ref, count_ref, sources)

    share = features // cycle
    total = lax.dot_general(attn_ref[...], cot_ref[...], (((0,), (0,)), ((), ())), preferred_element_type=jnp.float32)
    for d in range(cycle):
        gsend_ref[d] = total[d * share : (d + 1) * share].astype(jnp.bfloat16)
    shares = []
    for k, peer in enumerate(around):
        shares.append(remote(gsend_ref.at[peer], grecv_ref.at[k], share_send.at[k], share_recv.at[k],
                             {"space": peer}))
        shares[-1].start()
    out_ref[...] = (
        hid_ref[...].reshape(chunks * PATCH, features).astype(jnp.float32)
        + jnp.dot(attn_ref[...], weight_ref[7], preferred_element_type=jnp.float32)
    ).astype(jnp.bfloat16)
    gathered = gsend_ref[place].astype(jnp.float32)
    for k, step in enumerate(shares):
        step.wait_recv()
        gathered = gathered + grecv_ref[k].astype(jnp.float32)
    piece = share // levels
    for i in range(levels):
        lsend_ref[i] = gathered[i * piece : (i + 1) * piece].astype(jnp.bfloat16)
    parts = []
    for k, peer in enumerate(peers):
        parts.append(remote(lsend_ref.at[peer], lrecv_ref.at[k], part_send.at[k], part_recv.at[k], {"level": peer}))
        parts[-1].start()
    gathered = lsend_ref[level].astype(jnp.float32)
    for k, step in enumerate(parts):
        step.wait_recv()
        gathered = gathered + lrecv_ref[k].astype(jnp.float32)
    final_ref[level] = gathered.astype(jnp.bfloat16)
    fulls = []
    for k, peer in enumerate(peers):
        fulls.append(remote(final_ref.at[level], final_ref.at[level], full_send.at[k], full_recv.at[k],
                            {"level": peer}))
        fulls[-1].start()
    for step in fulls:
        step.wait_recv()
    for i in range(levels):
        grad_ref[i * piece : (i + 1) * piece, :] = final_ref[i].astype(jnp.float32)
    for steps in inward + back + halo + [shares, parts, fulls]:
        for step in steps:
            step.wait_send()


def body(fields, norm_vert, query_vert, keys_vert, values_vert, out_vert, level_bias, norm_patch, query_patch,
         keys_patch, values_patch, out_patch, patch_bias, neighbours, counts, cotangent):
    _, tokens, features = fields.shape
    levels = lax.axis_size("level")
    cycle = lax.axis_size("space")
    chunks = tokens // PATCH
    columns = PATCH // levels
    share = features // cycle
    x = fields.reshape(chunks, levels, columns, features)
    vmem = pl.BlockSpec(memory_space=pltpu.VMEM)
    smem = pl.BlockSpec(memory_space=pltpu.SMEM)
    hbm = pl.BlockSpec(memory_space=pl.ANY)
    narrow = lambda *shape: pltpu.VMEM(shape, jnp.bfloat16)
    dma = lambda *shape: pltpu.SemaphoreType.DMA(shape)
    blocks = 5 * chunks
    out, grad = pl.pallas_call(
        functools.partial(whole_kernel, cycle, levels),
        out_shape=(
            jax.ShapeDtypeStruct((tokens, features), jnp.bfloat16),
            jax.ShapeDtypeStruct((share, features), jnp.float32),
        ),
        in_specs=[vmem] * 3 + [hbm] * 9 + [smem] * 4,
        out_specs=(vmem, vmem),
        scratch_shapes=[
            narrow(8, features, features),
            narrow(tokens, features),
            narrow(chunks, levels, columns, features),
            narrow(chunks, levels, columns, features),
            narrow(chunks, levels, columns, features),
            narrow(tokens, features),
            narrow(chunks, PATCH, features),
            narrow(4 * chunks, PATCH, features),
            narrow(tokens, features),
            narrow(blocks, PATCH, features),
            narrow(blocks, PATCH, features),
            narrow(cycle, share, features),
            narrow(cycle - 1, share, features),
            narrow(levels, share // levels, features),
            narrow(levels - 1, share // levels, features),
            narrow(levels, share // levels, features),
            dma(9),
            dma(chunks, levels - 1),
            dma(chunks, levels - 1),
            dma(chunks, levels - 1),
            dma(chunks, levels - 1),
            dma(chunks, 4),
            dma(chunks, 4),
            dma(cycle - 1),
            dma(cycle - 1),
            dma(levels - 1),
            dma(levels - 1),
            dma(levels - 1),
            dma(levels - 1),
        ],
        compiler_params=pltpu.CompilerParams(
            collective_id=0, has_side_effects=True, vmem_limit_bytes=VMEM_LIMIT
        ),
        name="whole_block",
    )(x, norm_vert[None], norm_patch[None], query_vert, keys_vert, values_vert, out_vert, query_patch, keys_patch,
      values_patch, out_patch, cotangent[0], level_bias, patch_bias, neighbours, counts)
    return (out[None], grad)


def solution(mesh):
    split = P("level", "space", None)
    return jax.shard_map(
        body,
        mesh=mesh,
        in_specs=(split,) + (P(),) * 12 + (P("space", None), P("space"), split),
        out_specs=(split, P("space", None)),
        check_vma=False,
    )
```

time: 236 us -> 121 us (0.51)
  waiting for transfers between devices: 140 us -> 0 us
  Pallas kernels: 39.6 us -> 111 us
  blocking collectives: 23.3 us -> 0 us
  between operations: 14.1 us -> 0.65 us
  starting transfers between devices: 11 us -> 0 us
  local copies, waits for them, and re-layouts: 2.78 us -> 8.15 us
  other arithmetic: 5.07 us -> 0 us
    pallas_call x2 -> x1, Pallas kernels: 39.6 us -> 111 us  [body(): pl.pallas_call(functools.partial(whole_kernel, cycle, levels), out_shape=...]
    ppermute x4 -> x0, waiting for transfers between devices: 49.5 us -> none  [passed_along(): return lax.ppermute(value, axis, pairs)]
    psum x1 -> x0, waiting for transfers between devices: 36.8 us -> none  [body(): grad_wo = lax.psum(shares, 'level').astype(jnp.float32)]
    reduce_scatter x1 -> x0, waiting for transfers between devices: 34.9 us -> none  [body(): shares = lax.psum_scatter(grad, 'space', scatter_dimension=0, tiled=True)]
    all_to_all x1 -> x0, blocking collectives: 23.3 us -> none  [body(): lax.all_to_all(mixed, 'level', split_axis=0, concat_axis=0, tiled=True)]
    all_to_all x1 -> x0, waiting for transfers between devices: 18.9 us -> none  [body(): lax.all_to_all(split, 'level', split_axis=0, concat_axis=0, tiled=True)]
    all_to_all x1 -> x0, starting transfers between devices: 6.49 us -> none  [body(): lax.all_to_all(split, 'level', split_axis=0, concat_axis=0, tiled=True)]
    ppermute x4 -> x0, starting transfers between devices: 4.44 us -> none  [passed_along(): return lax.ppermute(value, axis, pairs)]
  transfers between devices with their start and end apart: 7 -> 0, of which waited for: 7 -> 0; matrix products, arithmetic and copies ran while one was open for 1% -> 0% of each run, Pallas kernels for 0% -> 0%
where the time goes in v2:
time: 121 us; the launch traced here: 120 us
  Pallas kernels  111 us (92%)
  local copies, waits for them, and re-layouts  8.15 us (7%)
    pallas_call x1, Pallas kernels, body(): pl.pallas_call(functools.partial(whole_kernel, cycle, levels), out_shape=...  111 us
    unnamed x6, local copies, waits for them, and re-layouts  5.59 us

profile of v2, /device:TPU:0, one launch (start us, length us, event | category | flops | bytes accessed | tf_op | source)
XLA Modules:
  0.0 120.2 jit_solution(14657990016257396479)
XLA Ops:
  0.6 1.3 %broadcast_in_dim.9.nv_ref = f32[1,768]{1,0:T(1,128)} reshape(f32[768]{0:T(1024)} %param.17) | data formatting | bytes 6144 | tf_op jit(solution)/shard_map/broadcast_in_dim | solution.py:332
  1.9 1.3 %broadcast_in_dim.10.np_ref = f32[1,768]{1,0:T(1,128)} reshape(f32[768]{0:T(1024)} %param.23) | data formatting | bytes 6144 | tf_op jit(solution)/shard_map/broadcast_in_dim | solution.py:332
  3.2 1.4 %copy.19.pb_ref = f32[12,2]{1,0:T(8,128)} copy(f32[12,2]{0,1:T(2,128)} %param.28) | data formatting | bytes 192 | tf_op args[12]
  4.6 1.4 %copy.18.lb_ref = f32[12,4,4]{2,1,0:T(4,128)} copy(f32[12,4,4]{0,2,1:T(4,128)} %param.22) | data formatting | bytes 1536 | tf_op args[6]
  6.0 111.4 %whole_block.1 = (bf16[512,768]{1,0:T(8,128)(2,1)}, f32[96,768]{1,0:T(8,128)}) custom-call(bf16[2,4,64,768]{3,2,1,0:T(8,128)(2,1)} %bitcast.3, f32[1,768]{1,0:T(1,128)} %broadcast_in_dim.9.nv_ref, f32[1,768]{1,0:T(1,128)} %broadcast_in_dim.10.np_ref, bf16[768,768]{1,0:T(8,128)(2,1)} %wqv_hbm.1, bf16[768,768]{1,0:T(8,128)(2,1)} %wkv_hbm.1, ...), custom_call_target="tpu_custom_call" | custom-call | tf_op jit(solution)/shard_map/whole_block/pallas_call | solution.py:289
  117.3 0.0 copy-start
  117.4 2.1 %copy.22 = bf16[1,512,768]{2,1,0:T(8,128)(2,1)} copy(bf16[1,512,768]{2,1,0:T(8,128)(2,1)} %bitcast.5) | data formatting | bytes 1572864
  119.5 0.0 copy-done
  119.5 0.7 copy.23
Async XLA Ops:
  117.3 2.1 %copy-start = (f32[96,768]{1,0:T(8,128)S(1)}, f32[96,768]{1,0:T(8,128)}, u32[]{:S(2)}) copy-start(f32[96,768]{1,0:T(8,128)} %get-tuple-element.9) | copy-start | bytes 884740

commit v3 on v2

--- a/solution.py
+++ b/solution.py
@@ -1,4 +1,5 @@
 import functools
+import math
 
 import jax
 import jax.numpy as jnp
@@ -10,6 +11,7 @@
 HD = 64
 PATCH = 256
 LANES = 128
+SPLIT = 2
 VMEM_LIMIT = 58 * 1024 * 1024
 
 epsilon = 1e-06
@@ -74,50 +76,41 @@
     return live, within
 
 
-def attend(q_ref, k_ref, v_ref, attn_ref, pb_ref, nb_ref, count_ref, sources):
-    tokens, features = q_ref.shape
-    per_device = tokens // PATCH
-    far = len(sources) * per_device
+def attend(step, q_ref, k_ref, v_ref, attn_ref, pb_ref, tables, far):
     low = lax.broadcasted_iota(jnp.int32, (1, LANES), 1) < HD
-    for patch in range(per_device):
+    lanes = pl.ds(pl.multiple_of(step * LANES, LANES), LANES)
+    for patch, picked in enumerate(tables):
         rows = pl.ds(patch * PATCH, PATCH)
-        picked = [choices(nb_ref, count_ref, patch, source, per_device) for source in sources]
-        blocks = [far + patch] + [o * per_device + within for o, (_, within) in enumerate(picked)]
-
-        def pair(step, carry):
-            lanes = pl.ds(pl.multiple_of(step * LANES, LANES), LANES)
-            query = q_ref[rows, lanes]
-            results = []
-            for parity in range(2):
-                head = step * 2 + parity
-                mine = low if parity == 0 else jnp.logical_not(low)
-                masked = jnp.where(mine, query, jnp.zeros_like(query))
-                scores = [
-                    lax.dot_general(
-                        masked, k_ref[block, :, lanes], (((1,), (1,)), ((), ())), preferred_element_type=jnp.float32
-                    )
-                    for block in blocks
-                ]
-                adds = [pb_ref[head, 0]] + [
-                    jnp.where(live > 0, pb_ref[head, 1], jnp.float32(-1e30)) for live, _ in picked
-                ]
-                top = functools.reduce(
-                    jnp.maximum, [jnp.max(s, axis=-1, keepdims=True) + a for s, a in zip(scores, adds)]
+        blocks = [far + patch] + [o * len(tables) + within for o, (_, within) in enumerate(picked)]
+        query = q_ref[rows, lanes]
+        results = []
+        for parity in range(2):
+            head = step * 2 + parity
+            mine = low if parity == 0 else jnp.logical_not(low)
+            masked = jnp.where(mine, query, jnp.zeros_like(query))
+            scores = [
+                lax.dot_general(
+                    masked, k_ref[block, :, lanes], (((1,), (1,)), ((), ())), preferred_element_type=jnp.float32
                 )
-                raised = [jnp.exp(s + (a - top)) for s, a in zip(scores, adds)]
-                total = functools.reduce(jnp.add, [jnp.sum(r, axis=-1, keepdims=True) for r in raised])
-                mixed = functools.reduce(
-                    jnp.add,
-                    [
-                        jnp.dot(r.astype(jnp.bfloat16), v_ref[block, :, lanes], preferred_element_type=jnp.float32)
-                        for r, block in zip(raised, blocks)
-                    ],
-                )
-                results.append(mixed / total)
-            attn_ref[rows, lanes] = jnp.where(low, results[0], results[1]).astype(jnp.bfloat16)
-            return carry
-
-        lax.fori_loop(0, features // LANES, pair, 0)
+                for block in blocks
+            ]
+            adds = [pb_ref[0, head]] + [
+                jnp.where(live > 0, pb_ref[1, head], jnp.float32(-1e30)) for live, _ in picked
+            ]
+            top = functools.reduce(
+                jnp.maximum, [jnp.max(s, axis=-1, keepdims=True) + a for s, a in zip(scores, adds)]
+            )
+            raised = [jnp.exp(s + (a - top)) for s, a in zip(scores, adds)]
+            total = functools.reduce(jnp.add, [jnp.sum(r, axis=-1, keepdims=True) for r in raised])
+            mixed = functools.reduce(
+                jnp.add,
+                [
+                    jnp.dot(r.astype(jnp.bfloat16), v_ref[block, :, lanes], preferred_element_type=jnp.float32)
+                    for r, block in zip(raised, blocks)
+                ],
+            )
+            results.append(mixed / total)
+        attn_ref[rows, lanes] = jnp.where(low, results[0], results[1]).astype(jnp.bfloat16)
 
 
 def remote(src, dst, send, recv, device):
@@ -150,8 +143,9 @@
         pl.semaphore_signal(barrier, inc=1, device_id={"space": peer}, device_id_type=pl.DeviceIdType.MESH)
     pl.semaphore_wait(barrier, levels - 1 + cycle - 1)
 
-    inward = []
-    for c in range(chunks):
+    inward, back, halo = [], [], []
+
+    def send_in(c):
         steps = []
         for k, peer in enumerate(peers):
             steps.append(remote(x_ref.at[c, peer], in_ref.at[c, level], in_send.at[c, k], in_recv.at[c, k],
@@ -160,23 +154,25 @@
         in_ref[c, level] = x_ref[c, level]
         inward.append(steps)
 
+    for c in range(min(2, chunks)):
+        send_in(c)
+
     lane = lax.broadcasted_iota(jnp.int32, (1, LANES), 1)
     bias_rows = []
     for i in range(levels):
         for j in range(levels):
             row = jnp.zeros((1, LANES), jnp.float32)
-            for h in range(lb_ref.shape[0]):
-                row = jnp.where(lane == h, lb_ref[h, i, j], row)
+            for h in range(lb_ref.shape[2]):
+                row = jnp.where(lane == h, lb_ref[i, j, h], row)
             bias_rows.append(row)
     for load in loads[:4]:
         load.wait()
 
-    back = []
-    for c in range(chunks):
+    def vertical_step(c):
         for step in inward[c]:
             step.wait_recv()
-        hsend_ref[c] = vertical(in_ref[c], nv_ref[...], weight_ref[0], weight_ref[1], weight_ref[2], weight_ref[3],
-                                bias_rows, attn_ref.at[pl.ds(0, PATCH)])
+        hsend_ref[c] = vertical(in_ref[c], nv_ref[...][None], weight_ref[0], weight_ref[1], weight_ref[2],
+                                weight_ref[3], bias_rows, attn_ref.at[pl.ds(0, levels * columns)])
         steps = []
         for k, peer in enumerate(peers):
             steps.append(remote(hsend_ref.at[c, peer], hid_ref.at[c, level], back_send.at[c, k], back_recv.at[c, k],
@@ -184,67 +180,123 @@
             steps[-1].start()
         hid_ref[c, level] = hsend_ref[c, level]
         back.append(steps)
-    for load in loads[4:]:
-        load.wait()
+        if c + 2 < chunks:
+            send_in(c + 2)
 
     toward = lax.rem(place, 2) * 2 - 1
     sources = [lax.rem(place + step * toward + 2 * cycle, cycle) for step in (1, 2, -1, -2)]
     partner = sources[2]
-    far = len(sources) * chunks
+    patches = chunks // SPLIT
+    far = len(sources) * patches
     scale = jnp.bfloat16(HD ** (-0.5))
-    halo = []
-    for c in range(chunks):
+
+    def halo_step(c):
         for step in back[c]:
             step.wait_recv()
-        normed = normalized(hid_ref[c].reshape(levels * columns, features).astype(jnp.float32), np_ref[...])
-        own_ref[c] = normed
+        own_ref[c] = normalized(
+            hid_ref[c].reshape(levels * columns, features).astype(jnp.float32), np_ref[...][None]
+        )
         steps = []
         for slot, target in ((0, sources[0]), (1, sources[3]), (2, partner)):
             steps.append(remote(own_ref.at[c], far_ref.at[slot * chunks + c], halo_send.at[c, slot],
                                 halo_recv.at[c, slot], {"space": target}))
             steps[-1].start()
         halo.append(steps)
-        q_ref[pl.ds(c * PATCH, PATCH), :] = project(normed, weight_ref[4]) * scale
-        k_ref[far + c] = project(normed, weight_ref[5])
-        v_ref[far + c] = project(normed, weight_ref[6])
-    def distant(block):
-        k_ref[block] = project(far_ref[block], weight_ref[5])
-        v_ref[block] = project(far_ref[block], weight_ref[6])
-
-    for c in range(chunks):
-        halo[c][2].wait_recv()
-        distant(2 * chunks + c)
+
+    def own_step(patch):
+        normed = own_ref[patch * SPLIT : (patch + 1) * SPLIT].reshape(PATCH, features)
+        q_ref[pl.ds(patch * PATCH, PATCH), :] = project(normed, weight_ref[4]) * scale
+        k_ref[far + patch] = project(normed, weight_ref[5])
+        v_ref[far + patch] = project(normed, weight_ref[6])
+
+    def forward(c):
         halo[c][0].wait_recv()
         passed = remote(far_ref.at[c], far_ref.at[3 * chunks + c], halo_send.at[c, 3], halo_recv.at[c, 3],
                         {"space": partner})
         passed.start()
         halo[c].append(passed)
-        distant(c)
-        halo[c][1].wait_recv()
-        distant(chunks + c)
+
+    def distant(slot, patch):
+        if slot:
+            for c in range(patch * SPLIT, (patch + 1) * SPLIT):
+                halo[c][slot].wait_recv()
+        start = slot * chunks + patch * SPLIT
+        block = far_ref[start : start + SPLIT].reshape(PATCH, features)
+        k_ref[slot * patches + patch] = project(block, weight_ref[5])
+        v_ref[slot * patches + patch] = project(block, weight_ref[6])
+
+    loaded = False
     for c in range(chunks):
-        halo[c][3].wait_recv()
-        distant(3 * chunks + c)
-
-    attend(q_ref, k_ref, v_ref, attn_ref, pb_ref, nb_ref, count_ref, sources)
+        vertical_step(c)
+        if c >= 1:
+            halo_step(c - 1)
+        if not loaded:
+            for load in loads[4:]:
+                load.wait()
+            loaded = True
+    for patch in range(patches - 1):
+        own_step(patch)
+        distant(2, patch)
+    halo_step(chunks - 1)
+    for c in range(chunks - SPLIT):
+        forward(c)
+    own_step(patches - 1)
+    for patch in range(patches - 1):
+        for slot in (0, 1, 3):
+            distant(slot, patch)
+    distant(2, patches - 1)
+    for c in range(chunks - SPLIT, chunks):
+        forward(c)
+    for slot in (0, 1, 3):
+        distant(slot, patches - 1)
 
     share = features // cycle
-    total = lax.dot_general(attn_ref[...], cot_ref[...], (((0,), (0,)), ((), ())), preferred_element_type=jnp.float32)
-    for d in range(cycle):
-        gsend_ref[d] = total[d * share : (d + 1) * share].astype(jnp.bfloat16)
-    shares = []
-    for k, peer in enumerate(around):
-        shares.append(remote(gsend_ref.at[peer], grecv_ref.at[k], share_send.at[k], share_recv.at[k],
-                             {"space": peer}))
-        shares[-1].start()
+    grain = gsend_ref.shape[1]
+    per_pair = LANES // grain
+    per_owner = share // grain
+    pairs = features // LANES
+    tables = [[choices(nb_ref, count_ref, patch, source, patches) for source in sources] for patch in range(patches)]
+
+    def share_of(index):
+        owner = index // per_owner
+        part = lax.rem(index, per_owner)
+        gap = lax.rem(place - owner + cycle, cycle)
+        slot = jnp.maximum(gap - 1, 0) * per_owner + part
+        return owner, remote(gsend_ref.at[index], grecv_ref.at[slot], share_send.at[index], share_recv.at[slot],
+                             {"space": owner})
+
+    def pair(turn, carry):
+        step = lax.rem(place * pairs // cycle + 1 + turn, pairs)
+        attend(step, q_ref, k_ref, v_ref, attn_ref, pb_ref, tables, far)
+        lanes = pl.ds(pl.multiple_of(step * LANES, LANES), LANES)
+        total = lax.dot_general(
+            attn_ref[:, lanes], cot_ref[...], (((0,), (0,)), ((), ())), preferred_element_type=jnp.float32
+        ).astype(jnp.bfloat16)
+        for part in range(per_pair):
+            gsend_ref[step * per_pair + part] = total[part * grain : (part + 1) * grain]
+        for part in range(per_pair):
+            owner, copy = share_of(step * per_pair + part)
+
+            @pl.when(owner != place)
+            def _():
+                copy.start()
+
+        return carry
+
+    lax.fori_loop(0, pairs, pair, 0)
     out_ref[...] = (
-        hid_ref[...].reshape(chunks * PATCH, features).astype(jnp.float32)
+        hid_ref[...].reshape(patches * PATCH, features).astype(jnp.float32)
         + jnp.dot(attn_ref[...], weight_ref[7], preferred_element_type=jnp.float32)
     ).astype(jnp.bfloat16)
-    gathered = gsend_ref[place].astype(jnp.float32)
-    for k, step in enumerate(shares):
-        step.wait_recv()
-        gathered = gathered + grecv_ref[k].astype(jnp.float32)
+    sums = []
+    for part in range(per_owner):
+        sums.append(gsend_ref[place * per_owner + part].astype(jnp.float32))
+        for k in range(cycle - 1):
+            slot = k * per_owner + part
+            remote(gsend_ref.at[0], grecv_ref.at[slot], share_send.at[0], share_recv.at[slot],
+                   {"space": partner}).wait_recv()
+            sums[-1] = sums[-1] + grecv_ref[slot].astype(jnp.float32)
+    gathered = jnp.concatenate(sums, axis=0)
     piece = share // levels
     for i in range(levels):
         lsend_ref[i] = gathered[i * piece : (i + 1) * piece].astype(jnp.bfloat16)
@@ -266,9 +318,20 @@
         step.wait_recv()
     for i in range(levels):
         grad_ref[i * piece : (i + 1) * piece, :] = final_ref[i].astype(jnp.float32)
-    for steps in inward + back + halo + [shares, parts, fulls]:
+    for steps in inward + back + halo + [parts, fulls]:
         for step in steps:
             step.wait_send()
+
+    def drained(index, carry):
+        owner, copy = share_of(index)
+
+        @pl.when(owner != place)
+        def _():
+            copy.wait_send()
+
+        return carry
+
+    lax.fori_loop(0, pairs * per_pair, drained, 0)
 
 
 def body(fields, norm_vert, query_vert, keys_vert, values_vert, out_vert, level_bias, norm_patch, query_patch,
@@ -276,8 +339,10 @@
     _, tokens, features = fields.shape
     levels = lax.axis_size("level")
     cycle = lax.axis_size("space")
-    chunks = tokens // PATCH
-    columns = PATCH // levels
+    patches = tokens // PATCH
+    chunks = patches * SPLIT
+    columns = PATCH // SPLIT // levels
+    grain = math.gcd(features // cycle, LANES)
     share = features // cycle
     x = fields.reshape(chunks, levels, columns, features)
     vmem = pl.BlockSpec(memory_space=pltpu.VMEM)
@@ -285,7 +350,7 @@
     hbm = pl.BlockSpec(memory_space=pl.ANY)
     narrow = lambda *shape: pltpu.VMEM(shape, jnp.bfloat16)
     dma = lambda *shape: pltpu.SemaphoreType.DMA(shape)
-    blocks = 5 * chunks
+    blocks = 5 * patches
     out, grad = pl.pallas_call(
         functools.partial(whole_kernel, cycle, levels),
         out_shape=(
@@ -301,13 +366,13 @@
             narrow(chunks, levels, columns, features),
             narrow(chunks, levels, columns, features),
             narrow(tokens, features),
-            narrow(chunks, PATCH, features),
-            narrow(4 * chunks, PATCH, features),
+            narrow(chunks, PATCH // SPLIT, features),
+            narrow(4 * chunks, PATCH // SPLIT, features),
             narrow(tokens, features),
             narrow(blocks, PATCH, features),
             narrow(blocks, PATCH, features),
-            narrow(cycle, share, features),
-            narrow(cycle - 1, share, features),
+            narrow(features // grain, grain, features),
+            narrow((cycle - 1) * share // grain, grain, features),
             narrow(levels, share // levels, features),
             narrow(levels - 1, share // levels, features),
             narrow(levels, share // levels, features),
@@ -318,8 +383,8 @@
             dma(chunks, levels - 1),
             dma(chunks, 4),
             dma(chunks, 4),
-            dma(cycle - 1),
-            dma(cycle - 1),
+            dma(features // grain),
+            dma((cycle - 1) * share // grain),
             dma(levels - 1),
             dma(levels - 1),
             dma(levels - 1),
@@ -329,8 +394,8 @@
             collective_id=0, has_side_effects=True, vmem_limit_bytes=VMEM_LIMIT
         ),
         name="whole_block",
-    )(x, norm_vert[None], norm_patch[None], query_vert, keys_vert, values_vert, out_vert, query_patch, keys_patch,
-      values_patch, out_patch, cotangent[0], level_bias, patch_bias, neighbours, counts)
+    )(x, norm_vert, norm_patch, query_vert, keys_vert, values_vert, out_vert, query_patch, keys_patch,
+      values_patch, out_patch, cotangent[0], jnp.transpose(level_bias, (1, 2, 0)), patch_bias.T, neighbours, counts)
     return (out[None], grad)
 
 

time: 121 us -> 96.3 us (0.80)
  Pallas kernels: 111 us -> 92.6 us
  local copies, waits for them, and re-layouts: 8.15 us -> 2.83 us
    pallas_call x1, Pallas kernels: 111 us -> 92.6 us  [body(): pl.pallas_call(functools.partial(whole_kernel, cycle, levels), out_shape=...]
    unnamed x6 -> x4, local copies, waits for them, and re-layouts: 5.59 us -> 2.83 us
    broadcast_in_dim x2 -> x0, local copies, waits for them, and re-layouts: 2.56 us -> none  [the longest x1 1.28 us: body(): norm_patch[None]]
where the time goes in v3:
time: 96.3 us; the launch traced here: 96.1 us
  Pallas kernels  92.6 us (96%)
  local copies, waits for them, and re-layouts  2.83 us (3%)
    pallas_call x1, Pallas kernels, body(): pl.pallas_call(functools.partial(whole_kernel, cycle, levels), out_shape=...  92.6 us
    unnamed x4, local copies, waits for them, and re-layouts  2.83 us

profile of v3, /device:TPU:0, one launch (start us, length us, event | category | flops | bytes accessed | tf_op | source)
XLA Modules:
  0.0 96.1 jit_solution(774222073995459087)
XLA Ops:
  0.6 92.6 %whole_block.1 = (bf16[512,768]{1,0:T(8,128)(2,1)}, f32[96,768]{1,0:T(8,128)}) custom-call(bf16[4,4,32,768]{3,2,1,0:T(8,128)(2,1)} %bitcast.5, f32[768]{0:T(1024)} %nv_ref.1, f32[768]{0:T(1024)} %np_ref.1, bf16[768,768]{1,0:T(8,128)(2,1)} %wqv_hbm.1, bf16[768,768]{1,0:T(8,128)(2,1)} %wkv_hbm.1, bf16[768,768]{1,0:T(8,128)(2,1)} %wvv_hbm.1, ...), custom_call_target="tpu_custom_call" | custom-call | tf_op jit(solution)/shard_map/whole_block/pallas_call | solution.py:354
  93.3 0.0 copy-start
  93.3 2.1 %copy.20 = bf16[1,512,768]{2,1,0:T(8,128)(2,1)} copy(bf16[1,512,768]{2,1,0:T(8,128)(2,1)} %bitcast.7) | data formatting | bytes 1572864
  95.4 0.0 copy-done
  95.4 0.7 copy.21
Async XLA Ops:
  93.3 2.1 %copy-start = (f32[96,768]{1,0:T(8,128)S(1)}, f32[96,768]{1,0:T(8,128)}, u32[]{:S(2)}) copy-start(f32[96,768]{1,0:T(8,128)} %get-tuple-element.9) | copy-start | bytes 884740

commit v4 on v3

--- a/solution.py
+++ b/solution.py
@@ -76,12 +76,14 @@
     return live, within
 
 
-def attend(step, q_ref, k_ref, v_ref, attn_ref, pb_ref, tables, far):
+def attend(step, q_ref, k_ref, v_ref, attn_ref, pb_ref, tables, far, slots, early, top_ref, total_ref, mixed_ref):
     low = lax.broadcasted_iota(jnp.int32, (1, LANES), 1) < HD
     lanes = pl.ds(pl.multiple_of(step * LANES, LANES), LANES)
     for patch, picked in enumerate(tables):
         rows = pl.ds(patch * PATCH, PATCH)
-        blocks = [far + patch] + [o * len(tables) + within for o, (_, within) in enumerate(picked)]
+        blocks = [slot * len(tables) + picked[slot][1] for slot in slots]
+        if early:
+            blocks = [far + patch] + blocks
         query = q_ref[rows, lanes]
         results = []
         for parity in range(2):
@@ -94,12 +96,15 @@
                 )
                 for block in blocks
             ]
-            adds = [pb_ref[0, head]] + [
-                jnp.where(live > 0, pb_ref[1, head], jnp.float32(-1e30)) for live, _ in picked
-            ]
+            adds = [jnp.where(picked[slot][0] > 0, pb_ref[1, head], jnp.float32(-1e30)) for slot in slots]
+            if early:
+                adds = [pb_ref[0, head]] + adds
             top = functools.reduce(
                 jnp.maximum, [jnp.max(s, axis=-1, keepdims=True) + a for s, a in zip(scores, adds)]
             )
+            if not early:
+                before = top_ref[rows, lanes][:, parity * HD : parity * HD + 1]
+                top = jnp.maximum(top, before)
             raised = [jnp.exp(s + (a - top)) for s, a in zip(scores, adds)]
             total = functools.reduce(jnp.add, [jnp.sum(r, axis=-1, keepdims=True) for r in raised])
             mixed = functools.reduce(
@@ -109,8 +114,17 @@
                     for r, block in zip(raised, blocks)
                 ],
             )
-            results.append(mixed / total)
-        attn_ref[rows, lanes] = jnp.where(low, results[0], results[1]).astype(jnp.bfloat16)
+            if early:
+                results.append((top, total, mixed))
+            else:
+                fade = jnp.exp(before - top)
+                total = total + total_ref[rows, lanes][:, parity * HD : parity * HD + 1] * fade
+                results.append((mixed + mixed_ref[rows, lanes] * fade) / total)
+        if early:
+            for ref, even, odd in zip((top_ref, total_ref, mixed_ref), *results):
+                ref[rows, lanes] = jnp.where(low, even, odd)
+        else:
+            attn_ref[rows, lanes] = jnp.where(low, results[0], results[1]).astype(jnp.bfloat16)
 
 
 def remote(src, dst, send, recv, device):
@@ -123,7 +137,7 @@
 def whole_kernel(cycle, levels, x_ref, nv_ref, np_ref, wqv_hbm, wkv_hbm, wvv_hbm, wov_hbm, wqp_hbm, wkp_hbm, wvp_hbm,
                  wop_hbm, cot_hbm, lb_ref, pb_ref, nb_ref, count_ref, out_ref, grad_ref, weight_ref, cot_ref, in_ref,
                  hsend_ref, hid_ref, attn_ref, own_ref, far_ref, q_ref, k_ref, v_ref, gsend_ref, grecv_ref, lsend_ref,
-                 lrecv_ref, final_ref, load_sem, in_send, in_recv, back_send, back_recv, halo_send, halo_recv,
+                 lrecv_ref, final_ref, top_ref, total_ref, mixed_ref, load_sem, in_send, in_recv, back_send, back_recv, halo_send, halo_recv,
                  share_send, share_recv, part_send, part_recv, full_send, full_recv):
     chunks, _, columns, features = x_ref.shape
     place = lax.axis_index("space")
@@ -241,12 +255,22 @@
     for c in range(chunks - SPLIT):
         forward(c)
     own_step(patches - 1)
+    distant(2, patches - 1)
     for patch in range(patches - 1):
         for slot in (0, 1, 3):
             distant(slot, patch)
-    distant(2, patches - 1)
-    for c in range(chunks - SPLIT, chunks):
+    pairs = features // LANES
+    tables = [[choices(nb_ref, count_ref, patch, source, patches) for source in sources] for patch in range(patches)]
+    states = (top_ref, total_ref, mixed_ref)
+
+    def early_pair(step, carry):
+        attend(step, q_ref, k_ref, v_ref, attn_ref, pb_ref, tables, far, (2,), True, *states)
+        return carry
+
+    for c in range(chunks - SPLIT, chunks - 1):
         forward(c)
+    lax.fori_loop(0, pairs, early_pair, 0)
+    forward(chunks - 1)
     for slot in (0, 1, 3):
         distant(slot, patches - 1)
 
@@ -254,8 +278,6 @@
     grain = gsend_ref.shape[1]
     per_pair = LANES // grain
     per_owner = share // grain
-    pairs = features // LANES
-    tables = [[choices(nb_ref, count_ref, patch, source, patches) for source in sources] for patch in range(patches)]
 
     def share_of(index):
         owner = index // per_owner
@@ -267,7 +289,7 @@
 
     def pair(turn, carry):
         step = lax.rem(place * pairs // cycle + 1 + turn, pairs)
-        attend(step, q_ref, k_ref, v_ref, attn_ref, pb_ref, tables, far)
+        attend(step, q_ref, k_ref, v_ref, attn_ref, pb_ref, tables, far, (0, 1, 3), False, *states)
         lanes = pl.ds(pl.multiple_of(step * LANES, LANES), LANES)
         total = lax.dot_general(
             attn_ref[:, lanes], cot_ref[...], (((0,), (0,)), ((), ())), preferred_element_type=jnp.float32
@@ -376,6 +398,9 @@
             narrow(levels, share // levels, features),
             narrow(levels - 1, share // levels, features),
             narrow(levels, share // levels, features),
+            pltpu.VMEM((tokens, features), jnp.float32),
+            pltpu.VMEM((tokens, features), jnp.float32),
+            pltpu.VMEM((tokens, features), jnp.float32),
             dma(9),
             dma(chunks, levels - 1),
             dma(chunks, levels - 1),

time: 96.3 us -> 94.8 us (0.984)
  Pallas kernels: 92.6 us -> 91.2 us
    pallas_call x1, Pallas kernels: 92.6 us -> 91.2 us  [body(): pl.pallas_call(functools.partial(whole_kernel, cycle, levels), out_shape=...]
where the time goes in v4:
time: 94.8 us; the launch traced here: 94.6 us
  Pallas kernels  91.2 us (96%)
  local copies, waits for them, and re-layouts  2.83 us (3%)
    pallas_call x1, Pallas kernels, body(): pl.pallas_call(functools.partial(whole_kernel, cycle, levels), out_shape=...  91.2 us
    unnamed x4, local copies, waits for them, and re-layouts  2.83 us

profile of v4, /device:TPU:0, one launch (start us, length us, event | category | flops | bytes accessed | tf_op | source)
XLA Modules:
  0.0 94.6 jit_solution(14524133215864026340)
XLA Ops:
  0.6 91.2 %whole_block.1 = (bf16[512,768]{1,0:T(8,128)(2,1)}, f32[96,768]{1,0:T(8,128)}) custom-call(bf16[4,4,32,768]{3,2,1,0:T(8,128)(2,1)} %bitcast.5, f32[768]{0:T(1024)} %nv_ref.1, f32[768]{0:T(1024)} %np_ref.1, bf16[768,768]{1,0:T(8,128)(2,1)} %wqv_hbm.1, bf16[768,768]{1,0:T(8,128)(2,1)} %wkv_hbm.1, bf16[768,768]{1,0:T(8,128)(2,1)} %wvv_hbm.1, ...), custom_call_target="tpu_custom_call" | custom-call | tf_op jit(solution)/shard_map/whole_block/pallas_call | solution.py:376
  91.8 0.0 copy-start
  91.8 2.1 %copy.20 = bf16[1,512,768]{2,1,0:T(8,128)(2,1)} copy(bf16[1,512,768]{2,1,0:T(8,128)(2,1)} %bitcast.7) | data formatting | bytes 1572864
  93.9 0.0 copy-done
  93.9 0.7 copy.21
Async XLA Ops:
  91.8 2.1 %copy-start = (f32[96,768]{1,0:T(8,128)S(1)}, f32[96,768]{1,0:T(8,128)}, u32[]{:S(2)}) copy-start(f32[96,768]{1,0:T(8,128)} %get-tuple-element.9) | copy-start | bytes 884740

commit v5 on v4

--- a/solution.py
+++ b/solution.py
@@ -338,8 +338,7 @@
         fulls[-1].start()
     for step in fulls:
         step.wait_recv()
-    for i in range(levels):
-        grad_ref[i * piece : (i + 1) * piece, :] = final_ref[i].astype(jnp.float32)
+    grad_ref[...] = final_ref[...]
     for steps in inward + back + halo + [parts, fulls]:
         for step in steps:
             step.wait_send()
@@ -377,7 +376,7 @@
         functools.partial(whole_kernel, cycle, levels),
         out_shape=(
             jax.ShapeDtypeStruct((tokens, features), jnp.bfloat16),
-            jax.ShapeDtypeStruct((share, features), jnp.float32),
+            jax.ShapeDtypeStruct((levels, share // levels, features), jnp.bfloat16),
         ),
         in_specs=[vmem] * 3 + [hbm] * 9 + [smem] * 4,
         out_specs=(vmem, vmem),
@@ -421,7 +420,7 @@
         name="whole_block",
     )(x, norm_vert, norm_patch, query_vert, keys_vert, values_vert, out_vert, query_patch, keys_patch,
       values_patch, out_patch, cotangent[0], jnp.transpose(level_bias, (1, 2, 0)), patch_bias.T, neighbours, counts)
-    return (out[None], grad)
+    return (out[None], grad.astype(jnp.float32).reshape(share, features))
 
 
 def solution(mesh):

time: 94.8 us -> 95.7 us (level)
  other arithmetic: 0 us -> 1.64 us
    reshape x0 -> x1, other arithmetic: none -> 1.64 us  [body(): return (out[None], grad.astype(jnp.float32).reshape(share, features))]
    unnamed x4 -> x1, local copies, waits for them, and re-layouts: 2.83 us -> 2.06 us
where the time goes in v5:
time: 95.7 us; the launch traced here: 95.5 us
  Pallas kernels  91.1 us (95%)
  local copies, waits for them, and re-layouts  2.06 us (2%)
  other arithmetic  1.64 us (2%)
    pallas_call x1, Pallas kernels, body(): pl.pallas_call(functools.partial(whole_kernel, cycle, levels), out_shape=...  91.1 us
    unnamed x1, local copies, waits for them, and re-layouts  2.06 us

profile of v5, /device:TPU:0, one launch (start us, length us, event | category | flops | bytes accessed | tf_op | source)
XLA Modules:
  0.0 95.5 jit_solution(13639767299178791304)
XLA Ops:
  0.6 91.1 %whole_block.1 = (bf16[512,768]{1,0:T(8,128)(2,1)}, bf16[4,24,768]{2,1,0:T(8,128)(2,1)}) custom-call(bf16[4,4,32,768]{3,2,1,0:T(8,128)(2,1)} %bitcast.8, f32[768]{0:T(1024)} %nv_ref.1, f32[768]{0:T(1024)} %np_ref.1, bf16[768,768]{1,0:T(8,128)(2,1)} %wqv_hbm.1, bf16[768,768]{1,0:T(8,128)(2,1)} %wkv_hbm.1, bf16[768,768]{1,0:T(8,128)(2,1)} %wvv_hbm.1, ...), custom_call_target="tpu_custom_call" | custom-call | tf_op jit(solution)/shard_map/whole_block/pallas_call | solution.py:375
  91.8 1.6 %bitcast_convert_fusion = f32[96,768]{1,0:T(8,128)} fusion(bf16[4,24,768]{2,1,0:T(8,128)(2,1)} %get-tuple-element.5), kind=kLoop, calls=%fused_computation | loop fusion | flops 73728 | bytes 442368 | tf_op jit(solution)/shard_map/reshape | solution.py:423
  93.4 2.1 %copy.19 = bf16[1,512,768]{2,1,0:T(8,128)(2,1)} copy(bf16[1,512,768]{2,1,0:T(8,128)(2,1)} %bitcast.10) | data formatting | bytes 1572864
